TPU v7x, 256 devices: a whole 4x4x8 slice. The times are simulated.
256 devices in a mesh: rep: 8 (over y, z_lo), dp: 32 (over x, z_hi, core).
Axes of the slice: x: 4, y: 4, z: 8 (z_hi: 4, z_lo: 2; z = z_hi * 2 + z_lo), core: 2. Of those that a mesh axis runs over, the one named last changes fastest.
Arguments:
- images: bfloat16 [2048, 2, 1280], P(('rep', 'dp')), may hold values from -6 to 6
- weight: bfloat16 [1280, 8192], P(None, 'dp'), may hold values from -0.3354102 to 0.3354102, as said below
Outputs:
- image_grad: float32 [2048, 2, 1280], P(('rep', 'dp'))
- weight_grad: float32 [1280, 8192], P(None, 'dp')
Inputs may be any that keep to these rules, and one draw needn't show every extreme that they name: `weight`: a projection whose columns have different scales.
All inputs are finite; a program needn't handle non-finite values.
Results may differ from a plain program's by a relative error of at most 0.0021.
Values may be sent and summed in bfloat16 or wider, within the bound.
A program may use at most 64 MiB of HBM per device.

v0:
```python
import jax
import jax.numpy as jnp
from jax import lax
from jax.sharding import Mesh
from jax.sharding import PartitionSpec as P

DP = ("dp_0", "dp_1", "dp_2")
REP_DP = ("rep", "dp_0", "dp_1", "dp_2")


invariance_weight = 25.0
variance_weight = 25.0
covariance_weight = 1.0
loss_scale = 8192.0
epsilon_var = 0.0001


def cut_along(shard, dim, peers):
    before, after = (shard.shape[:dim], shard.shape[dim + 1 :])
    return jnp.moveaxis(shard.reshape(*before, peers, -1, *after), dim, 0)


def sent_and_summed(shard, axis, dim):
    peers = lax.axis_size(axis)
    tiles = lax.all_to_all(cut_along(shard, dim, peers), axis, 0, 0, tiled=True)
    return jnp.sum(tiles, axis=0)


def sum_by_axis(shard, axes, dim):
    far, near = axes
    tiles = cut_along(shard, dim, lax.axis_size(far))
    nearer = sent_and_summed(tiles, near, dim + 1)
    arrived = lax.all_to_all(nearer, far, split_axis=0, concat_axis=0, tiled=True)
    return arrived.sum(axis=0)


def filled_up(lines, peers):
    spare = -len(lines) % peers
    return jnp.pad(lines, [(0, spare)] + [(0, 0)] * (lines.ndim - 1))


def sent_to_all(shard, axis):
    copies = jnp.broadcast_to(shard, (lax.axis_size(axis), *shard.shape))
    return lax.all_to_all(copies, axis, split_axis=0, concat_axis=0, tiled=True)


def in_order(tiles, dim):
    tiles = jnp.moveaxis(tiles, 0, dim)
    shape = tiles.shape
    return tiles.reshape(*shape[:dim], shape[dim] * shape[dim + 1], *shape[dim + 2 :])


def whole_of(shard, axes, dim):
    far, near = axes
    tiles = sent_to_all(sent_to_all(shard, far), near)
    return in_order(tiles.swapaxes(0, 1).reshape(-1, *shard.shape), dim)


def nested_sum(shard, axes):
    lines = shard.reshape(-1, shard.shape[-1])
    own = sum_by_axis(filled_up(lines, lax.axis_size(axes[0]) * lax.axis_size(axes[1])), axes, 0)
    whole = whole_of(own, axes, 0)
    return whole[: len(lines)].reshape(shard.shape)


def shards(images, weight):
    groups = lax.axis_size("rep")
    owners = lax.axis_size(DP)
    block_width = weight.shape[1]
    features = block_width * owners
    rows_all = lax.all_gather(images, DP, axis=0, tiled=True)
    zblock = jnp.einsum("mvk,ki->mvi", rows_all, weight, preferred_element_type=jnp.float32)
    count = zblock.shape[0]
    grad_scale = loss_scale / groups
    column_mean = jnp.mean(zblock, axis=0)
    centred = zblock - column_mean
    centred_bf = centred.astype(jnp.bfloat16)
    variance = jnp.sum(centred * centred, axis=0) / (count - 1)
    spread = jnp.sqrt(variance + epsilon_var)
    coeff = grad_scale * 4.0 * covariance_weight / (features * (count - 1))
    gram_part = jnp.einsum(
        "mvi,nvi->vmn", centred_bf, centred_bf, preferred_element_type=jnp.float32
    )
    gram = nested_sum(gram_part, (("dp_0", "dp_1"), "dp_2"))
    centred_wide = centred_bf.astype(jnp.float32)
    diag_cov = jnp.sum(centred_wide * centred_wide, axis=0) / (count - 1)
    through = jnp.einsum("vmn,nvi->mvi", gram, centred_wide, precision=lax.Precision.HIGHEST)
    cov_term = through * (coeff / (count - 1)) - coeff * diag_cov * centred_wide
    view_gap = zblock[:, 0] - zblock[:, 1]
    inv_term = jnp.stack([view_gap, -view_gap], axis=1) * (
        grad_scale * 2.0 * invariance_weight / (count * features)
    )
    var_term = (
        jnp.where(
            spread < 1.0, -grad_scale * variance_weight / (features * (count - 1)) / spread, 0.0
        )
        * centred
    )
    feature_grad = (inv_term + var_term + cov_term).astype(jnp.bfloat16)
    local_grad = jnp.einsum(
        "mvk,mvi->ki", rows_all, feature_grad, preferred_element_type=jnp.float32
    )
    weight_grad = lax.psum(local_grad, "rep")
    image_grad = lax.psum_scatter(
        jnp.einsum("mvi,ki->mvk", feature_grad, weight, preferred_element_type=jnp.float32),
        DP,
        scatter_dimension=0,
        tiled=True,
    )
    return (image_grad, weight_grad)


def solution(mesh):
    finer = Mesh(mesh.devices.reshape(mesh.shape["rep"], 4, 4, 2), ("rep", "dp_0", "dp_1", "dp_2"))
    return jax.shard_map(
        shards,
        mesh=finer,
        in_specs=(P(REP_DP, None, None), P(None, DP)),
        out_specs=(P(REP_DP, None, None), P(None, DP)),
        check_vma=False,
    )
```

profile of v0, /device:TPU:8, one launch (start us, length us, event | category | flops | bytes accessed | tf_op | source)
XLA Modules:
  0.0 303.5 jit_solution(8967959175923659122)
XLA Ops:
  7.2 0.0 copy-start
  7.2 0.0 all-gather.2.cloned.1.call-start
  7.2 1.5 copy.18
  8.7 0.0 all-gather.2.cloned.1.call-update
  8.7 57.8 %all-gather.2.cloned.1.call-done = bf16[256,2,1280]{2,0,1:T(8,128)(2,1)} async-done(((bf16[8,2,1280]{2,0,1:T(8,128)(2,1)}), bf16[256,2,1280]{2,0,1:T(8,128)(2,1)}) %all-gather.2.cloned.1.call-update) | async-done | bytes 1310736 | tf_op jit(solution)/shard_map/all_gather | solution.py:71
  66.5 0.0 copy-done
  66.6 1.8 fusion.12
  68.4 0.3 fusion.10
  68.7 4.2 %all_to_all.20 = f32[2,16,16,256]{3,2,1,0:T(8,128)S(1)} all-to-all(f32[2,16,16,256]{3,2,1,0:T(8,128)S(1)} %bitcast.30), channel_id=1, replica_groups=mesh['rep'=8,'dp_0'=4,'dp_1'=4,'dp_2'=2] {'dp_2'}, dimensions={0} | all-to-all | bytes 1048576 | tf_op jit(solution)/shard_map/all_to_all | solution.py:25
  72.9 18.8 %all_to_all.21 = f32[16,16,256]{2,1,0:T(8,128)S(1)} all-to-all(f32[16,16,256]{2,1,0:T(8,128)S(1)} %reduce_sum.47), channel_id=1, replica_groups=mesh['rep'=8,'dp_0'=4,'dp_1'=4,'dp_2'=2] {'dp_0','dp_1'}, dimensions={0} | all-to-all | bytes 524288 | tf_op jit(solution)/shard_map/all_to_all | solution.py:33
  91.8 0.7 broadcast_in_dim.14
  92.5 3.5 %all-to-all-start.2 = ((f32[16,16,256]{2,1,0:T(8,128)}), f32[16,16,256]{2,1,0:T(8,128)S(1)}, u32[]{:S(2)}, u32[]{:S(2)}) async-start(f32[16,16,256]{2,1,0:T(8,128)} %broadcast_in_dim.14), calls=%async_computation.2 | async-start | bytes 524288 | tf_op jit(solution)/shard_map/all_to_all | solution.py:44
  96.0 0.0 all-reduce.2.cloned.1.call-start
  96.1 0.1 multiply_reduce_fusion
  96.2 12.9 %all-to-all-done.2 = f32[16,16,256]{2,1,0:T(8,128)S(1)} async-done(((f32[16,16,256]{2,1,0:T(8,128)}), f32[16,16,256]{2,1,0:T(8,128)S(1)}, u32[]{:S(2)}, u32[]{:S(2)}) %all-to-all-start.2) | async-done | bytes 262176 | tf_op jit(solution)/shard_map/all_to_all | solution.py:44
  109.2 0.1 broadcast_in_dim.15
  109.2 4.2 %all_to_all.22 = f32[2,16,16,256]{3,2,1,0:T(8,128)S(1)} all-to-all(f32[2,16,16,256]{3,2,1,0:T(8,128)S(1)} %broadcast_in_dim.15), channel_id=1, replica_groups=mesh['rep'=8,'dp_0'=4,'dp_1'=4,'dp_2'=2] {'dp_2'}, dimensions={0} | all-to-all | bytes 1048576 | tf_op jit(solution)/shard_map/all_to_all | solution.py:44
  113.4 0.0 copy-start.1
  113.4 0.5 fusion.3
  113.9 0.8 copy-done.1
  114.7 1.6 convolution_bitcast_fusion
  116.3 0.0 all-reduce.2.cloned.1.call-update
  116.3 0.0 reduce-scatter.2.cloned.1.call-start
  116.4 2.0 fusion.4
  118.4 0.0 reduce-scatter.2.cloned.1.call-update
  118.4 78.9 %all-reduce.2.cloned.1.call-done = f32[1280,256]{0,1:T(8,128)} async-done(((f32[1280,256]{0,1:T(8,128)}), f32[1280,256]{0,1:T(8,128)}) %all-reduce.2.cloned.1.call-update) | async-done | bytes 1310736 | tf_op jit(solution)/shard_map/psum | solution.py:103
  197.4 2.8 copy.25
  200.2 95.3 %reduce-scatter.2.cloned.1.call-done = f32[8,2,1280]{2,0,1:T(8,128)} async-done(((f32[256,2,1280]{2,0,1:T(8,128)}), f32[8,2,1280]{2,0,1:T(8,128)}) %reduce-scatter.2.cloned.1.call-update) | async-done | bytes 81936 | tf_op jit(solution)/shard_map/reduce_scatter | solution.py:104
  295.5 1.6 copy.24
  (7 shorter events, 0.2 us)
Async XLA Ops:
  7.2 59.4 %copy-start = (bf16[1280,256]{1,0:T(8,128)(2,1)S(1)}, bf16[1280,256]{1,0:T(8,128)(2,1)}, u32[]{:S(2)}) copy-start(bf16[1280,256]{1,0:T(8,128)(2,1)} %param.3) | copy-start | bytes 1966084
  7.2 59.4 %all-gather.2.cloned.1.call-start = ((), (), s32[]{:S(2)}) async-start(), calls=%async_computation.5 | async-start | bytes 1351680 | tf_op jit(solution)/shard_map/all_gather | solution.py:71
  92.5 16.7 %all-to-all-start.2 = ((f32[16,16,256]{2,1,0:T(8,128)}), f32[16,16,256]{2,1,0:T(8,128)S(1)}, u32[]{:S(2)}, u32[]{:S(2)}) async-start(f32[16,16,256]{2,1,0:T(8,128)} %broadcast_in_dim.14), calls=%async_computation.2 | async-start | bytes 524288 | tf_op jit(solution)/shard_map/all_to_all | solution.py:44
  96.0 101.3 %all-reduce.2.cloned.1.call-start = ((), (), s32[]{:S(2)}) async-start(), calls=%async_computation.7 | async-start | bytes 2621440 | tf_op jit(solution)/shard_map/psum | solution.py:103
  113.4 1.3 copy-start.1
  116.3 179.1 %reduce-scatter.2.cloned.1.call-start = ((), (), s32[]{:S(2)}) async-start(), calls=%async_computation.6 | async-start | bytes 2703360 | tf_op jit(solution)/shard_map/reduce_scatter | solution.py:104
Sparse Core Ops, SparseCore 0:
  11.2 55.2 all-gather.1
  116.4 80.8 all-reduce.1
  201.2 94.1 reduce-scatter.1
where the time goes:
time: 304 us
  waiting for transfers between devices  245 us (81%)
  blocking collectives  27.1 us (9%)
  between operations  13.8 us (5%)
  local copies, waits for them, and re-layouts  7.46 us (2%)
  matrix products  6.2 us (2%)
  starting transfers between devices  3.67 us (1%)
    reduce_scatter x1, waiting for transfers between devices, shards(): lax.psum_scatter(jnp.einsum('mvi,ki->mvk', feature_grad, weight, preferre...  95.3 us
    psum x1, waiting for transfers between devices, shards(): weight_grad = lax.psum(local_grad, 'rep')  78.9 us
    all_gather x1, waiting for transfers between devices, shards(): rows_all = lax.all_gather(images, DP, axis=0, tiled=True)  57.8 us
    all_to_all x1, blocking collectives, sum_by_axis(): lax.all_to_all(nearer, far, split_axis=0, concat_axis=0, tiled=True)  18.8 us
    all_to_all x1, waiting for transfers between devices, sent_to_all(): return lax.all_to_all(copies, axis, split_axis=0, concat_axis=0, tiled=True)  12.9 us
    unnamed x7, local copies, waits for them, and re-layouts  6.6 us
  transfers between devices with their start and end apart: 4, of which 4 were waited for; matrix products, arithmetic and copies ran while one was open for 2% of the time, Pallas kernels for 0%

commit v1 on v0

v1 whole, which is shorter than its diff:
```python
import jax
import jax.numpy as jnp
from jax import lax
from jax.experimental import pallas as pl
from jax.experimental.pallas import tpu as pltpu
from jax.sharding import PartitionSpec as P

MESH = pl.DeviceIdType.MESH
F32, BF16 = jnp.float32, jnp.bfloat16

N_REP, N_DP = 8, 32
M = 256
D_IN = 1280
BLOCK = 256
EMB = BLOCK * N_DP
S = 8192.0 / N_REP
EPS = 0.0001
INV = S * 2.0 * 25.0 / (M * EMB)
VAR = S * 25.0 / (EMB * (M - 1))
COV = S * 4.0 / (EMB * (M - 1))
CHUNKS = 2
WIDE = BLOCK // CHUNKS


def enc(v):
    return (v * jnp.abs(v)).astype(BF16)


def dec(b):
    t = b.astype(F32)
    s = jnp.sqrt(jnp.abs(t))
    return jnp.where(t < 0.0, -s, s)


def nt(a, b):
    return lax.dot_general(a, b, (((1,), (1,)), ((), ())), preferred_element_type=F32)


def tn(a, b):
    return lax.dot_general(a, b, (((0,), (0,)), ((), ())), preferred_element_type=F32)


def nn(a, b):
    return jnp.dot(a, b, preferred_element_type=F32)


def kernel(
    img, w, ig, wg,
    sw, X, Xo, Wo, E, Cb, base,
    T, Tx, Sz, Szr, TA,
    Ff, Fo,
    Pc, P0, Px, S32, Pz, Pzr, R, Rr,
    L32, Lc, Ly, Lz, Lzr, LA,
    send, recv,
):
    rep, dp = lax.axis_index("rep"), lax.axis_index("dp")
    y, zl = rep // 2, rep % 2
    c, chip = dp % 2, dp // 2
    x, zh = chip // 4, chip % 4

    partner = (rep, chip * 2 + (1 - c))

    def at_x(k):
        return (rep, (((x + k) % 4) * 4 + zh) * 2 + c)

    def at_z(k):
        return (rep, (x * 4 + (zh + k) % 4) * 2 + c)

    def at_y(k):
        return (((y + k) % 4) * 2 + zl, dp)

    across = (y * 2 + (1 - zl), dp)

    barrier = pltpu.get_barrier_semaphore()
    peers = [partner, across]
    for k in (1, 2, 3):
        peers += [at_x(k), at_z(k), at_y(k)]
    for peer in peers:
        pl.semaphore_signal(barrier, inc=1, device_id=peer, device_id_type=MESH)
    pl.semaphore_wait(barrier, len(peers))

    started = []

    def put(src, dst, device):
        i = len(started)
        copy = pltpu.make_async_remote_copy(
            src_ref=src, dst_ref=dst, send_sem=send.at[i], recv_sem=recv.at[i],
            device_id=device, device_id_type=MESH,
        )
        copy.start()
        started.append(copy)
        return copy

    swap = put(img.at[1 - c], sw, partner)
    wswap = put(w, Wo, partner)
    own = img[c]
    swap.wait_recv()
    other = sw[...]
    first = c == 0
    X[chip] = jnp.concatenate([jnp.where(first, own, other), jnp.where(first, other, own)], axis=0)
    zs = [put(X.at[chip], X.at[chip], at_z(k)) for k in (1, 2, 3)]
    xs = []
    for k in range(4):
        if k:
            zs[k - 1].wait_recv()
        slot = x * 4 + (zh - k + 4) % 4
        xs += [put(X.at[slot], X.at[slot], at_x(j)) for j in (1, 2, 3)]
    for copy in xs:
        copy.wait_recv()
    xswap = put(X, Xo, partner)

    rows = X[...].reshape(M, D_IN)
    wswap.wait_recv()
    for h, wr in enumerate((w, Wo)):
        e = nn(rows, wr[...])
        E[h] = e
        Cb[:, h * BLOCK:(h + 1) * BLOCK] = (e - jnp.mean(e, axis=0, keepdims=True)).astype(BF16)
    top = nt(Cb[0:128, :], Cb[...])
    low = nt(Cb[128:256, :], Cb[128:256, :])
    T[:, :, 0:256] = top.reshape(4, 32, 256)
    T[:, :, 256:384] = low.reshape(4, 32, 128)
    ts = [put(T.at[(x + k) % 4], Tx.at[k - 1], at_x(k)) for k in (1, 2, 3)]
    for copy in ts:
        copy.wait_recv()
    Sz[...] = T[x] + Tx[0] + Tx[1] + Tx[2]
    ss = [put(Sz, Szr.at[k - 1], at_z(k)) for k in (1, 2, 3)]

    xswap.wait_recv()
    orows = Xo[...].reshape(M, D_IN)
    for h, wr in enumerate((w, Wo)):
        e = E[h]
        gap = e - nn(orows, wr[...])
        centred = e - jnp.mean(e, axis=0, keepdims=True)
        spread = jnp.sqrt(jnp.sum(centred * centred, axis=0, keepdims=True) / (M - 1) + EPS)
        pull = jnp.where(spread < 1.0, -VAR / spread, 0.0)
        cb = Cb[:, h * BLOCK:(h + 1) * BLOCK].astype(F32)
        diag = jnp.sum(cb * cb, axis=0, keepdims=True) / (M - 1)
        base[h] = INV * gap + pull * centred - (COV * diag) * cb

    for copy in ss:
        copy.wait_recv()
    TA[x] = Sz[...] + Szr[0] + Szr[1] + Szr[2]
    gs = [put(TA.at[x], TA.at[x], at_x(k)) for k in (1, 2, 3)]
    for copy in gs:
        copy.wait_recv()
    top = TA[:, :, 0:256].reshape(128, 256)
    low = TA[:, :, 256:384].reshape(128, 128)
    gram = jnp.concatenate([top, jnp.concatenate([top[:, 128:256].T, low], axis=1)], axis=0)
    hi = gram.astype(BF16)
    lo = (gram - hi.astype(F32)).astype(BF16)
    for h in (1, 0):
        cb = Cb[:, h * BLOCK:(h + 1) * BLOCK]
        through = nn(hi, cb) + nn(lo, cb)
        Ff[h] = (base[h] + through * (COV / (M - 1))).astype(BF16)
        if h == 1:
            fswap = put(Ff.at[1], Fo, partner)

    ps = []
    for k in (2, 1, 3, 0):
        at = pl.ds(pl.multiple_of(((x + k) % 4) * 64, 64), 64)
        part = (nt(Ff[0, at, :], w[...]) + nt(Ff[1, at, :], Wo[...])).reshape(4, 16, D_IN)
        if k:
            Pc[k - 1] = enc(part)
            ps.append(put(Pc.at[k - 1], Px.at[k - 1], at_x(k)))
        else:
            P0[...] = part

    fswap.wait_recv()
    for j in range(5):
        cols = pl.ds(j * 256, 256)
        L32[cols, :] = tn(X[:, :, cols].reshape(M, 256), Ff[0]) + tn(Xo[:, :, cols].reshape(M, 256), Fo[...])
    ys = []
    for h in range(CHUNKS):
        lanes = pl.ds(h * WIDE, WIDE)
        for k in (2, 1, 3):
            at = pl.ds(pl.multiple_of(((y + k) % 4) * 320, 320), 320)
            Lc[h, k - 1] = enc(L32[at, lanes])
            ys.append(put(Lc.at[h, k - 1], Ly.at[h, k - 1], at_y(k)))

    for copy in ps:
        copy.wait_recv()
    for j in range(4):
        s = P0[j] + dec(Px[0, j]) + dec(Px[1, j]) + dec(Px[2, j])
        S32[j] = s
        Pz[j] = enc(s)
    pz = [put(Pz.at[(zh + k) % 4], Pzr.at[k - 1], at_z(k)) for k in (2, 1, 3)]

    mine = pl.ds(pl.multiple_of(y * 320, 320), 320)
    zz = []
    for h in range(CHUNKS):
        for copy in ys[3 * h:3 * h + 3]:
            copy.wait_recv()
        lanes = pl.ds(h * WIDE, WIDE)
        s = L32[mine, lanes] + dec(Ly[h, 0]) + dec(Ly[h, 1]) + dec(Ly[h, 2])
        Lz[h] = enc(s)
        zz.append(put(Lz.at[h], Lzr.at[h], across))

    for copy in pz:
        copy.wait_recv()
    r = S32[zh] + dec(Pzr[0]) + dec(Pzr[1]) + dec(Pzr[2])
    R[...] = r.reshape(2, 8, D_IN)
    rswap = put(R.at[1 - c], Rr, partner)

    ls = []
    for h in range(CHUNKS):
        zz[h].wait_recv()
        LA[h, y] = enc(dec(Lz[h]) + dec(Lzr[h]))
        ls += [put(LA.at[h, y], LA.at[h, y], at_y(k)) for k in (2, 1, 3)]

    rswap.wait_recv()
    ig[c] = R[c]
    ig[1 - c] = Rr[...]

    for h in range(CHUNKS):
        for copy in ls[3 * h:3 * h + 3]:
            copy.wait_recv()
        for j in range(4):
            wg[j * 320:(j + 1) * 320, h * WIDE:(h + 1) * WIDE] = dec(LA[h, j])
    for copy in started:
        copy.wait_send()


def shards(images, weight):
    V = pltpu.VMEM
    ig, wg = pl.pallas_call(
        kernel,
        out_shape=(
            jax.ShapeDtypeStruct((2, 8, D_IN), F32),
            jax.ShapeDtypeStruct((D_IN, BLOCK), F32),
        ),
        in_specs=[pl.BlockSpec(memory_space=V)] * 2,
        out_specs=[pl.BlockSpec(memory_space=V)] * 2,
        scratch_shapes=[
            V((8, D_IN), BF16),
            V((16, 16, D_IN), BF16),
            V((16, 16, D_IN), BF16),
            V((D_IN, BLOCK), BF16),
            V((2, M, BLOCK), F32),
            V((M, 2 * BLOCK), BF16),
            V((2, M, BLOCK), F32),
            V((4, 32, 384), F32),
            V((3, 32, 384), F32),
            V((32, 384), F32),
            V((3, 32, 384), F32),
            V((4, 32, 384), F32),
            V((2, M, BLOCK), BF16),
            V((M, BLOCK), BF16),
            V((3, 4, 16, D_IN), BF16),
            V((4, 16, D_IN), F32),
            V((3, 4, 16, D_IN), BF16),
            V((4, 16, D_IN), F32),
            V((4, 16, D_IN), BF16),
            V((3, 16, D_IN), BF16),
            V((2, 8, D_IN), F32),
            V((8, D_IN), F32),
            V((D_IN, BLOCK), F32),
            V((CHUNKS, 3, 320, WIDE), BF16),
            V((CHUNKS, 3, 320, WIDE), BF16),
            V((CHUNKS, 320, WIDE), BF16),
            V((CHUNKS, 320, WIDE), BF16),
            V((CHUNKS, 4, 320, WIDE), BF16),
            pltpu.SemaphoreType.DMA((64,)),
            pltpu.SemaphoreType.DMA((64,)),
        ],
        compiler_params=pltpu.CompilerParams(
            collective_id=0, has_side_effects=True, vmem_limit_bytes=60 * 2**20
        ),
    )(images.transpose(1, 0, 2), weight)
    return ig.transpose(1, 0, 2), wg


def solution(mesh):
    return jax.shard_map(
        shards,
        mesh=mesh,
        in_specs=(P(("rep", "dp"), None, None), P(None, "dp")),
        out_specs=(P(("rep", "dp"), None, None), P(None, "dp")),
        check_vma=False,
    )
```

time: 304 us -> 71.4 us (0.23)
  waiting for transfers between devices: 245 us -> 0 us
  Pallas kernels: 0 us -> 63.9 us
  blocking collectives: 27.1 us -> 0 us
  between operations: 13.8 us -> 0.64 us
  matrix products: 6.2 us -> 0 us
  starting transfers between devices: 3.67 us -> 0 us
    reduce_scatter x1 -> x0, waiting for transfers between devices: 95.3 us -> none  [shards(): lax.psum_scatter(jnp.einsum('mvi,ki->mvk', feature_grad, weight, preferre...]
    psum x1 -> x0, waiting for transfers between devices: 78.9 us -> none  [shards(): weight_grad = lax.psum(local_grad, 'rep')]
    pallas_call x0 -> x1, Pallas kernels: none -> 63.9 us  [shards(): pl.pallas_call(kernel, out_shape=(jax.ShapeDtypeStruct((2, 8, D_IN), F32)...]
    all_gather x1 -> x0, waiting for transfers between devices: 57.8 us -> none  [shards(): rows_all = lax.all_gather(images, DP, axis=0, tiled=True)]
    all_to_all x3 -> x0, blocking collectives: 27.1 us -> none  [the longest x1 18.8 us: sum_by_axis(): lax.all_to_all(nearer, far, split_axis=0, concat_axis=0, tiled=True)]
    all_to_all x1 -> x0, waiting for transfers between devices: 12.9 us -> none  [sent_to_all(): return lax.all_to_all(copies, axis, split_axis=0, concat_axis=0, tiled=True)]
    dot_general x5 -> x0, matrix products: 6.2 us -> none  [the longest x1 2.05 us: shards(): jnp.einsum('mvi,ki->mvk', feature_grad, weight, preferred_element_type=jn...]
    all_to_all x1 -> x0, starting transfers between devices: 3.55 us -> none  [sent_to_all(): return lax.all_to_all(copies, axis, split_axis=0, concat_axis=0, tiled=True)]
  transfers between devices with their start and end apart: 4 -> 0, of which waited for: 4 -> 0; matrix products, arithmetic and copies ran while one was open for 2% -> 0% of each run, Pallas kernels for 0% -> 0%
where the time goes in v1:
time: 71.4 us; the launch traced here: 70 us
  Pallas kernels  63.9 us (89%)
  local copies, waits for them, and re-layouts  5.42 us (8%)
    pallas_call x1, Pallas kernels, shards(): pl.pallas_call(kernel, out_shape=(jax.ShapeDtypeStruct((2, 8, D_IN), F32)...  63.9 us
    unnamed x3, local copies, waits for them, and re-layouts  5.42 us

profile of v1, /device:TPU:8, one launch (start us, length us, event | category | flops | bytes accessed | tf_op | source)
XLA Modules:
  0.0 70.0 jit_solution(849831062446163886)
XLA Ops:
  0.6 1.4 %copy.7 = bf16[8,2,1280]{2,0,1:T(8,128)(2,1)} copy(bf16[8,2,1280]{2,1,0:T(2,128)(2,1)} %param.2) | data formatting | bytes 81920 | tf_op args[0]
  2.0 63.9 %shard_map.41 = (f32[2,8,1280]{2,1,0:T(8,128)}, f32[1280,256]{1,0:T(8,128)}) custom-call(bf16[2,8,1280]{2,1,0:T(8,128)(2,1)} %bitcast.4, bf16[1280,256]{1,0:T(8,128)(2,1)} %w.1), custom_call_target="tpu_custom_call" | custom-call | tf_op jit(solution)/shard_map/pallas_call | solution.py:225
  66.0 1.6 %copy.5 = f32[8,2,1280]{2,1,0:T(2,128)} copy(f32[8,2,1280]{2,0,1:T(8,128)} %bitcast.5) | data formatting | bytes 163840
  67.5 2.5 %copy.9 = f32[1280,256]{1,0:T(8,128)} copy(f32[1280,256]{1,0:T(8,128)} %get-tuple-element.11) | data formatting | bytes 2621440

commit v2 on v1

v2 whole, which is shorter than its diff:
```python
import jax
import jax.numpy as jnp
from jax import lax
from jax.experimental import pallas as pl
from jax.experimental.pallas import tpu as pltpu
from jax.sharding import PartitionSpec as P

MESH = pl.DeviceIdType.MESH
F32, BF16 = jnp.float32, jnp.bfloat16

N_REP, N_DP = 8, 32
M = 256
D_IN = 1280
BLOCK = 256
EMB = BLOCK * N_DP
S = 8192.0 / N_REP
EPS = 0.0001
INV = S * 2.0 * 25.0 / (M * EMB)
VAR = S * 25.0 / (EMB * (M - 1))
COV = S * 4.0 / (EMB * (M - 1))
CHUNKS = 2
WIDE = BLOCK // CHUNKS
CUT = 1024
REST = D_IN - CUT
GRAM_UNIT = 2.0**-10


def root(t):
    return jnp.sqrt(jnp.abs(t))


def enc(v):
    return (v * jnp.abs(v)).astype(BF16)


def dec(b):
    t = b.astype(F32)
    s = root(t)
    return jnp.where(t < 0.0, -s, s)


def enc4(g):
    v = g * GRAM_UNIT
    return ((v * jnp.abs(v)) * (v * v)).astype(BF16)


def dec4(b):
    t = b.astype(F32)
    s = root(root(t)) * (1.0 / GRAM_UNIT)
    return jnp.where(t < 0.0, -s, s)


def nt(a, b):
    return lax.dot_general(a, b, (((1,), (1,)), ((), ())), preferred_element_type=F32)


def tn(a, b):
    return lax.dot_general(a, b, (((0,), (0,)), ((), ())), preferred_element_type=F32)


def nn(a, b):
    return jnp.dot(a, b, preferred_element_type=F32)


def kernel(
    img, w, ig, lg,
    I2, X, Xo, Wo, WT, E, Cb, base,
    T, Tc, Tx, Sz, Sc, Szr, TA,
    Ff, Fo,
    Pc, P0, Px, S32, Pz, Pzr,
    B32, Bc, Bz, B2, Bx, Bxr, R, Rr,
    L32, Lc, Ly, Lz, Lzr, La,
    send, recv, local,
):
    rep, dp = lax.axis_index("rep"), lax.axis_index("dp")
    y, zl = rep // 2, rep % 2
    c, chip = dp % 2, dp // 2
    x, zh = chip // 4, chip % 4
    o = 1 - c

    partner = (rep, chip * 2 + o)

    def at_x(k, core):
        return (rep, (((x + k) % 4) * 4 + zh) * 2 + core)

    def at_z(k, core):
        return (rep, (x * 4 + (zh + k) % 4) * 2 + core)

    def at_y(k):
        return (((y + k) % 4) * 2 + zl, dp)

    across = (y * 2 + (1 - zl), dp)

    barrier = pltpu.get_barrier_semaphore()
    peers = [partner, across]
    for k in (1, 2, 3):
        peers += [at_x(k, c), at_z(k, c), at_x(k, o), at_z(k, o), at_y(k)]
    for peer in peers:
        pl.semaphore_signal(barrier, inc=1, device_id=peer, device_id_type=MESH)
    both = img[...].astype(F32)
    I2[0] = both[:, 0, :].astype(BF16)
    I2[1] = both[:, 1, :].astype(BF16)
    pl.semaphore_wait(barrier, len(peers))

    started = []

    def put(src, dst, device):
        i = len(started)
        copy = pltpu.make_async_remote_copy(
            src_ref=src, dst_ref=dst, send_sem=send.at[i], recv_sem=recv.at[i],
            device_id=device, device_id_type=MESH,
        )
        copy.start()
        started.append(copy)
        return copy

    at = pl.ds(pl.multiple_of(c * 8, 8), 8)
    A, B = pl.ds(0, CUT), pl.ds(CUT, REST)
    az, bx = [], []
    for k in (2, 1, 3):
        for core in (c, o):
            az.append(put(I2.at[core, :, A], X.at[chip, at, A], at_z(k, core)))
            bx.append(put(I2.at[core, :, B], X.at[chip, at, B], at_x(k, core)))
    mate = put(I2.at[o], X.at[chip, at], partner)
    keep = pltpu.make_async_copy(I2.at[c], X.at[chip, at], local.at[0])
    keep.start()
    wswap = put(w, Wo, partner)
    keep.wait()
    mate.wait_recv()
    forwards = []
    for k in (0, 1, 3, 2):
        if k:
            j = (2, 1, 3).index(k) * 2
            az[j].wait_recv()
            az[j + 1].wait_recv()
        slot = x * 4 + (zh - k + 4) % 4
        forwards += [put(X.at[slot, :, A], X.at[slot, :, A], at_x(j, c)) for j in (2, 1, 3)]
        if k:
            j = (2, 1, 3).index(k) * 2
            bx[j].wait_recv()
            bx[j + 1].wait_recv()
        slot = ((x - k + 4) % 4) * 4 + zh
        forwards += [put(X.at[slot, :, B], X.at[slot, :, B], at_z(j, c)) for j in (2, 1, 3)]
    wswap.wait_recv()
    WT[0] = w[...].T
    WT[1] = Wo[...].T
    for copy in forwards:
        copy.wait_recv()
    xswap = put(X, Xo, partner)

    rows = X[...].reshape(M, D_IN)
    for h, wr in enumerate((w, Wo)):
        e = nn(rows, wr[...])
        E[h] = e
        Cb[:, h * BLOCK:(h + 1) * BLOCK] = (e - jnp.mean(e, axis=0, keepdims=True)).astype(BF16)
    top = nt(Cb[0:128, :], Cb[...])
    low = nt(Cb[128:256, :], Cb[128:256, :])
    T[:, :, 0:256] = top.reshape(4, 32, 256)
    T[:, :, 256:384] = low.reshape(4, 32, 128)
    Tc[:, :, 0:256] = enc4(top).reshape(4, 32, 256)
    Tc[:, :, 256:384] = enc4(low).reshape(4, 32, 128)
    ts = [put(Tc.at[(x + k) % 4], Tx.at[k - 1], at_x(k, c)) for k in (2, 1, 3)]
    for copy in ts:
        copy.wait_recv()
    s = T[x] + dec4(Tx[0]) + dec4(Tx[1]) + dec4(Tx[2])
    Sz[...] = s
    Sc[...] = enc4(s)
    ss = [put(Sc, Szr.at[k - 1], at_z(k, c)) for k in (2, 1, 3)]

    xswap.wait_recv()
    orows = Xo[...].reshape(M, D_IN)
    for h, wr in enumerate((w, Wo)):
        e = E[h]
        gap = e - nn(orows, wr[...])
        centred = e - jnp.mean(e, axis=0, keepdims=True)
        spread = jnp.sqrt(jnp.sum(centred * centred, axis=0, keepdims=True) / (M - 1) + EPS)
        pull = jnp.where(spread < 1.0, -VAR / spread, 0.0)
        cb = Cb[:, h * BLOCK:(h + 1) * BLOCK].astype(F32)
        diag = jnp.sum(cb * cb, axis=0, keepdims=True) / (M - 1)
        base[h] = INV * gap + pull * centred - (COV * diag) * cb

    for copy in ss:
        copy.wait_recv()
    TA[x] = enc4(Sz[...] + dec4(Szr[0]) + dec4(Szr[1]) + dec4(Szr[2]))
    gs = [put(TA.at[x], TA.at[x], at_x(k, c)) for k in (2, 1, 3)]
    for copy in gs:
        copy.wait_recv()
    top = dec4(TA[:, :, 0:256].reshape(128, 256))
    low = dec4(TA[:, :, 256:384].reshape(128, 128))
    gram = jnp.concatenate([top, jnp.concatenate([top[:, 128:256].T, low], axis=1)], axis=0)
    hi = gram.astype(BF16)
    lo = (gram - hi.astype(F32)).astype(BF16)
    for h in (1, 0):
        cb = Cb[:, h * BLOCK:(h + 1) * BLOCK]
        through = nn(hi, cb) + nn(lo, cb)
        Ff[h] = (base[h] + through * (COV / (M - 1))).astype(BF16)
        if h == 1:
            fswap = put(Ff.at[1], Fo, partner)

    ps = []
    for k in (2, 1, 3, 0):
        at = pl.ds(pl.multiple_of(((x + k) % 4) * 64, 64), 64)
        part = (nn(Ff[0, at, :], WT[0, :, 0:CUT]) + nn(Ff[1, at, :], WT[1, :, 0:CUT])).reshape(4, 16, CUT)
        if k:
            Pc[k - 1] = enc(part)
            ps.append(put(Pc.at[k - 1], Px.at[k - 1], at_x(k, c)))
        else:
            P0[...] = part
    part = (nn(Ff[0], WT[0, :, CUT:D_IN]) + nn(Ff[1], WT[1, :, CUT:D_IN])).reshape(4, 4, 16, REST)
    for j in range(4):
        B32[j] = part[:, j]
        Bc[j] = enc(part[:, j])
    bz = [put(Bc.at[(zh + k) % 4], Bz.at[k - 1], at_z(k, c)) for k in (2, 1, 3)]

    fswap.wait_recv()
    for j in range(5):
        cols = pl.ds(j * 256, 256)
        L32[cols, :] = tn(X[:, :, cols].reshape(M, 256), Ff[0]) + tn(Xo[:, :, cols].reshape(M, 256), Fo[...])
    ys = []
    for h in range(CHUNKS):
        lanes = pl.ds(h * WIDE, WIDE)
        for k in (2, 1, 3):
            at = pl.ds(pl.multiple_of(((y + k) % 4) * 320, 320), 320)
            Lc[h, k - 1] = enc(L32[at, lanes])
            ys.append(put(Lc.at[h, k - 1], Ly.at[h, k - 1], at_y(k)))

    for copy in bz:
        copy.wait_recv()
    for j in range(4):
        s = B32[zh, j] + dec(Bz[0, j]) + dec(Bz[1, j]) + dec(Bz[2, j])
        B2[j] = s
        Bx[j] = enc(s)
    bs = [put(Bx.at[(x + k) % 4], Bxr.at[k - 1], at_x(k, c)) for k in (2, 1, 3)]

    for copy in ps:
        copy.wait_recv()
    for j in range(4):
        s = P0[j] + dec(Px[0, j]) + dec(Px[1, j]) + dec(Px[2, j])
        S32[j] = s
        Pz[j] = enc(s)
    pz = [put(Pz.at[(zh + k) % 4], Pzr.at[k - 1], at_z(k, c)) for k in (2, 1, 3)]

    mine = pl.ds(pl.multiple_of(y * 320, 320), 320)
    zz = []
    for h in range(CHUNKS):
        for copy in ys[3 * h:3 * h + 3]:
            copy.wait_recv()
        lanes = pl.ds(h * WIDE, WIDE)
        s = L32[mine, lanes] + dec(Ly[h, 0]) + dec(Ly[h, 1]) + dec(Ly[h, 2])
        Lz[h] = enc(s)
        zz.append(put(Lz.at[h], Lzr.at[h], across))

    ls, kept = [], []
    for h in range(CHUNKS):
        zz[h].wait_recv()
        La[h] = enc(dec(Lz[h]) + dec(Lzr[h]))
        there = lg.at[mine, pl.ds(h * WIDE, WIDE)]
        ls += [put(La.at[h], there, at_y(k)) for k in (2, 1, 3)]
        kept.append(pltpu.make_async_copy(La.at[h], there, local.at[1 + h]))
        kept[-1].start()

    for copy in pz + bs:
        copy.wait_recv()
    r = S32[zh] + dec(Pzr[0]) + dec(Pzr[1]) + dec(Pzr[2])
    R[:, :, 0:CUT] = r.reshape(2, 8, CUT)
    r = B2[x] + dec(Bxr[0]) + dec(Bxr[1]) + dec(Bxr[2])
    R[:, :, CUT:D_IN] = r.reshape(2, 8, REST)
    rswap = put(R.at[o], Rr, partner)
    rswap.wait_recv()
    own, other = R[c], Rr[...]
    first = c == 0
    ig[:, 0, :] = jnp.where(first, own, other)
    ig[:, 1, :] = jnp.where(first, other, own)

    for copy in ls:
        copy.wait_recv()
    for copy in kept:
        copy.wait()
    for copy in started:
        copy.wait_send()


def shards(images, weight):
    V = pltpu.VMEM
    ig, lg = pl.pallas_call(
        kernel,
        out_shape=(
            jax.ShapeDtypeStruct((8, 2, D_IN), F32),
            jax.ShapeDtypeStruct((D_IN, BLOCK), BF16),
        ),
        in_specs=[pl.BlockSpec(memory_space=V)] * 2,
        out_specs=[pl.BlockSpec(memory_space=V), pl.BlockSpec(memory_space=LGSPACE)],
        scratch_shapes=[
            V((2, 8, D_IN), BF16),
            V((16, 16, D_IN), BF16),
            V((16, 16, D_IN), BF16),
            V((D_IN, BLOCK), BF16),
            V((2, BLOCK, D_IN), BF16),
            V((2, M, BLOCK), F32),
            V((M, 2 * BLOCK), BF16),
            V((2, M, BLOCK), F32),
            V((4, 32, 384), F32),
            V((4, 32, 384), BF16),
            V((3, 32, 384), BF16),
            V((32, 384), F32),
            V((32, 384), BF16),
            V((3, 32, 384), BF16),
            V((4, 32, 384), BF16),
            V((2, M, BLOCK), BF16),
            V((M, BLOCK), BF16),
            V((3, 4, 16, CUT), BF16),
            V((4, 16, CUT), F32),
            V((3, 4, 16, CUT), BF16),
            V((4, 16, CUT), F32),
            V((4, 16, CUT), BF16),
            V((3, 16, CUT), BF16),
            V((4, 4, 16, REST), F32),
            V((4, 4, 16, REST), BF16),
            V((3, 4, 16, REST), BF16),
            V((4, 16, REST), F32),
            V((4, 16, REST), BF16),
            V((3, 16, REST), BF16),
            V((2, 8, D_IN), F32),
            V((8, D_IN), F32),
            V((D_IN, BLOCK), F32),
            V((CHUNKS, 3, 320, WIDE), BF16),
            V((CHUNKS, 3, 320, WIDE), BF16),
            V((CHUNKS, 320, WIDE), BF16),
            V((CHUNKS, 320, WIDE), BF16),
            V((CHUNKS, 320, WIDE), BF16),
            pltpu.SemaphoreType.DMA((96,)),
            pltpu.SemaphoreType.DMA((96,)),
            pltpu.SemaphoreType.DMA((4,)),
        ],
        compiler_params=pltpu.CompilerParams(
            collective_id=0, has_side_effects=True, vmem_limit_bytes=VLIM
        ),
    )(images, weight)
    return ig, dec(lg)


LGSPACE = pl.ANY
VLIM = 24 * 2**20


def solution(mesh):
    return jax.shard_map(
        shards,
        mesh=mesh,
        in_specs=(P(("rep", "dp"), None, None), P(None, "dp")),
        out_specs=(P(("rep", "dp"), None, None), P(None, "dp")),
        check_vma=False,
    )
```

time: 71.4 us -> 63.1 us (0.88); the launches traced: 70 us -> 62.9 us
  Pallas kernels: 63.9 us -> 58.2 us
  local copies, waits for them, and re-layouts: 5.42 us -> 2.49 us
  other arithmetic: 0 us -> 1.57 us
    pallas_call x1, Pallas kernels: 63.9 us -> 58.2 us  [shards(): pl.pallas_call(kernel, out_shape=(jax.ShapeDtypeStruct((8, 2, D_IN), F32)...]
    unnamed x3 -> x5, local copies, waits for them, and re-layouts: 5.42 us -> 2.49 us
    select_n x0 -> x1, other arithmetic: none -> 1.57 us  [dec(): return jnp.where(t < 0.0, -s, s)]
where the time goes in v2:
time: 63.1 us; the launch traced here: 62.9 us
  Pallas kernels  58.2 us (92%)
  local copies, waits for them, and re-layouts  2.49 us (4%)
  other arithmetic  1.57 us (2%)
  between operations  0.65 us (1%)
    pallas_call x1, Pallas kernels, shards(): pl.pallas_call(kernel, out_shape=(jax.ShapeDtypeStruct((8, 2, D_IN), F32)...  58.2 us
    unnamed x5, local copies, waits for them, and re-layouts  2.49 us
    select_n x1, other arithmetic, dec(): return jnp.where(t < 0.0, -s, s)  1.57 us

profile of v2, /device:TPU:8, one launch (start us, length us, event | category | flops | bytes accessed | tf_op | source)
XLA Modules:
  0.0 62.9 jit_solution(6658196087943645322)
XLA Ops:
  0.6 0.0 copy-start
  0.6 1.1 %copy-done = bf16[1280,256]{1,0:T(8,128)(2,1)S(1)} copy-done((bf16[1280,256]{1,0:T(8,128)(2,1)S(1)}, bf16[1280,256]{1,0:T(8,128)(2,1)}, u32[]{:S(2)}) %copy-start) | copy-done | bytes 655384
  1.7 0.0 copy-start.1
  1.7 0.8 %copy-done.1 = bf16[8,2,1280]{2,1,0:T(2,128)(2,1)S(1)} copy-done((bf16[8,2,1280]{2,1,0:T(2,128)(2,1)S(1)}, bf16[8,2,1280]{2,1,0:T(2,128)(2,1)}, u32[]{:S(2)}) %copy-start.1) | copy-done | bytes 40984
  2.5 58.2 %shard_map.41 = (f32[8,2,1280]{2,1,0:T(2,128)S(1)}, bf16[1280,256]{1,0:T(8,128)(2,1)S(1)}) custom-call(bf16[8,2,1280]{2,1,0:T(2,128)(2,1)S(1)} %copy-done.1, bf16[1280,256]{1,0:T(8,128)(2,1)S(1)} %copy-done), custom_call_target="tpu_custom_call" | custom-call | tf_op jit(solution)/shard_map/pallas_call | solution.py:285
  60.7 1.6 %negate_select_fusion = f32[1280,256]{1,0:T(8,128)} fusion(bf16[1280,256]{1,0:T(8,128)(2,1)S(1)} %get-tuple-element.5), kind=kLoop, calls=%fused_computation | loop fusion | flops 1638400 | bytes 1966080 | tf_op jit(solution)/shard_map/jit(_where)/select_n | solution.py:39
  62.3 0.6 %copy.5 = f32[8,2,1280]{2,1,0:T(2,128)} copy(f32[8,2,1280]{2,1,0:T(2,128)S(1)} %get-tuple-element.8) | data formatting | bytes 163840
Async XLA Ops:
  0.6 1.1 %copy-start = (bf16[1280,256]{1,0:T(8,128)(2,1)S(1)}, bf16[1280,256]{1,0:T(8,128)(2,1)}, u32[]{:S(2)}) copy-start(bf16[1280,256]{1,0:T(8,128)(2,1)} %w.1) | copy-start | bytes 1966084
  1.7 0.8 %copy-start.1 = (bf16[8,2,1280]{2,1,0:T(2,128)(2,1)S(1)}, bf16[8,2,1280]{2,1,0:T(2,128)(2,1)}, u32[]{:S(2)}) copy-start(bf16[8,2,1280]{2,1,0:T(2,128)(2,1)} %img.1) | copy-start | bytes 122884

commit v3 on v2

v3 whole, which is shorter than its diff:
```python
import jax
import jax.numpy as jnp
from jax import lax
from jax.experimental import pallas as pl
from jax.experimental.pallas import tpu as pltpu
from jax.sharding import PartitionSpec as P

MESH = pl.DeviceIdType.MESH
F32, BF16 = jnp.float32, jnp.bfloat16

N_REP, N_DP = 8, 32
M = 256
D_IN = 1280
BLOCK = 256
EMB = BLOCK * N_DP
S = 8192.0 / N_REP
EPS = 0.0001
INV = S * 2.0 * 25.0 / (M * EMB)
VAR = S * 25.0 / (EMB * (M - 1))
COV = S * 4.0 / (EMB * (M - 1))
CHUNKS = 4
ROWS = D_IN // 4 // CHUNKS
CUT = 1024
REST = D_IN - CUT
GRAM_UNIT = 2.0**-10


def root(t):
    return jnp.sqrt(jnp.abs(t))


def enc(v):
    return (v * jnp.abs(v)).astype(BF16)


def dec(b):
    t = b.astype(F32)
    s = root(t)
    return jnp.where(t < 0.0, -s, s)


def enc4(g):
    v = g * GRAM_UNIT
    return ((v * jnp.abs(v)) * (v * v)).astype(BF16)


def dec4(b):
    t = b.astype(F32)
    s = root(root(t)) * (1.0 / GRAM_UNIT)
    return jnp.where(t < 0.0, -s, s)


def nt(a, b):
    return lax.dot_general(a, b, (((1,), (1,)), ((), ())), preferred_element_type=F32)


def tn(a, b):
    return lax.dot_general(a, b, (((0,), (0,)), ((), ())), preferred_element_type=F32)


def nn(a, b):
    return jnp.dot(a, b, preferred_element_type=F32)


class Group:
    def __init__(self, sem):
        self.sem, self.kib = sem, 0


def kernel(
    img, w_hbm, ig, lg,
    Iv, w, I2, X, Xo, Wo, WT, E, Cb, base,
    T, Tc, Tx, Sz, Sc, Szr, TA, Dg, Dx, Ds, Dz,
    Ff, Fo,
    Pc, P0, Px, S32, Pz, Pzr,
    B32, Bc, Bz, B2, Bx, Bxr, R, Rr,
    L32, Lo, Ld, Lc, Ro, Rd, Rc, Lz, Lzr, La,
    span, send, recv, local,
):
    rep, dp = lax.axis_index("rep"), lax.axis_index("dp")
    y, zl = rep // 2, rep % 2
    c, chip = dp % 2, dp // 2
    x, zh = chip // 4, chip % 4
    o = 1 - c

    partner = (rep, chip * 2 + o)

    def at_x(k, core):
        return (rep, (((x + k) % 4) * 4 + zh) * 2 + core)

    def at_z(k, core):
        return (rep, (x * 4 + (zh + k) % 4) * 2 + core)

    def at_y(k):
        return (((y + k) % 4) * 2 + zl, dp)

    across = (y * 2 + (1 - zl), dp)

    fetch = pltpu.make_async_copy(img, Iv, local.at[0])
    fetch.start()
    wfetch = pltpu.make_async_copy(w_hbm, w, local.at[1])
    wfetch.start()
    barrier = pltpu.get_barrier_semaphore()
    peers = [partner, across]
    for k in (1, 2, 3):
        peers += [at_x(k, c), at_z(k, c), at_x(k, o), at_z(k, o), at_y(k)]
    for peer in peers:
        pl.semaphore_signal(barrier, inc=1, device_id=peer, device_id_type=MESH)
    fetch.wait()
    both = Iv[...].astype(F32)
    I2[0] = both[:, 0, :].astype(BF16)
    I2[1] = both[:, 1, :].astype(BF16)
    pl.semaphore_wait(barrier, len(peers))

    sent = Group(send)
    groups = []

    def group():
        groups.append(Group(recv.at[len(groups)]))
        return groups[-1]

    def put(src, dst, device, at=None):
        at = at or group()
        copy = pltpu.make_async_remote_copy(
            src_ref=src, dst_ref=dst, send_sem=sent.sem, recv_sem=at.sem,
            device_id=device, device_id_type=MESH,
        )
        copy.start()
        size = 1
        for n in src.shape:
            size *= n
        kib = size * jnp.dtype(src.dtype).itemsize // 1024
        at.kib += kib
        sent.kib += kib
        return at

    def wait(at):
        part = span.at[pl.ds(0, at.kib * 2)]
        pltpu.make_async_copy(part, part, at.sem).wait()

    at = pl.ds(pl.multiple_of(c * 8, 8), 8)
    A, B = pl.ds(0, CUT), pl.ds(CUT, REST)
    az, bx = {}, {}
    for k in (1, 3, 2):
        az[k], bx[k] = group(), group()
        for core in (c, o):
            put(I2.at[core, :, A], X.at[chip, at, A], at_z(k, core), az[k])
            put(I2.at[core, :, B], X.at[chip, at, B], at_x(k, core), bx[k])
    mate = put(I2.at[o], X.at[chip, at], partner)
    keep = pltpu.make_async_copy(I2.at[c], X.at[chip, at], local.at[0])
    keep.start()
    wswap = put(w_hbm, Wo, partner)
    keep.wait()
    wait(mate)
    forwards = group()
    for k in (0, 1, 3, 2):
        if k:
            wait(az[k])
        slot = x * 4 + (zh - k + 4) % 4
        for j in (2, 1, 3):
            put(X.at[slot, :, A], X.at[slot, :, A], at_x(j, c), forwards)
        if k:
            wait(bx[k])
        slot = ((x - k + 4) % 4) * 4 + zh
        for j in (2, 1, 3):
            put(X.at[slot, :, B], X.at[slot, :, B], at_z(j, c), forwards)
    wait(wswap)
    wfetch.wait()
    WT[0] = w[...].T
    WT[1] = Wo[...].T
    wait(forwards)
    xswap = put(X, Xo, partner)

    rows = X[...].reshape(M, D_IN)
    for h, wr in enumerate((w, Wo)):
        e = nn(rows, wr[...])
        E[h] = e
        Cb[:, h * BLOCK:(h + 1) * BLOCK] = (e - jnp.mean(e, axis=0, keepdims=True)).astype(BF16)
    ri = lax.broadcasted_iota(jnp.int32, (128, 128), 0)
    ci = lax.broadcasted_iota(jnp.int32, (128, 128), 1)
    top = nt(Cb[0:128, :], Cb[...])
    low = nt(Cb[128:256, :], Cb[128:256, :])
    mixed = jnp.where(ri <= ci, top[:, 0:128], low)
    T[:, :, 0:128] = mixed.reshape(4, 32, 128)
    T[:, :, 128:256] = top[:, 128:256].reshape(4, 32, 128)
    Tc[...] = enc4(T[...])
    diags = [jnp.sum(jnp.where(ri == ci, g, 0.0), axis=0, keepdims=True) for g in (top[:, 0:128], low)]
    Dg[...] = jnp.where(lax.broadcasted_iota(jnp.int32, (8, 128), 0) == 0, diags[0], diags[1])
    ts = group()
    for k in (2, 1, 3):
        put(Tc.at[(x + k) % 4], Tx.at[k - 1], at_x(k, c), ts)
        put(Dg, Dx.at[k - 1], at_x(k, c), ts)
    wait(ts)
    s = T[x] + dec4(Tx[0]) + dec4(Tx[1]) + dec4(Tx[2])
    Sz[...] = s
    Sc[...] = enc4(s)
    Ds[...] = Dg[...] + Dx[0] + Dx[1] + Dx[2]
    ss = group()
    for k in (2, 1, 3):
        put(Sc, Szr.at[k - 1], at_z(k, c), ss)
        put(Ds, Dz.at[k - 1], at_z(k, c), ss)

    wait(xswap)
    orows = Xo[...].reshape(M, D_IN)
    for h, wr in enumerate((w, Wo)):
        e = E[h]
        gap = e - nn(orows, wr[...])
        centred = e - jnp.mean(e, axis=0, keepdims=True)
        spread = jnp.sqrt(jnp.sum(centred * centred, axis=0, keepdims=True) / (M - 1) + EPS)
        pull = jnp.where(spread < 1.0, -VAR / spread, 0.0)
        cb = Cb[:, h * BLOCK:(h + 1) * BLOCK].astype(F32)
        diag = jnp.sum(cb * cb, axis=0, keepdims=True) / (M - 1)
        base[h] = INV * gap + pull * centred - (COV * diag) * cb

    wait(ss)
    TA[x] = enc4(Sz[...] + dec4(Szr[0]) + dec4(Szr[1]) + dec4(Szr[2]))
    gs = group()
    for k in (2, 1, 3):
        put(TA.at[x], TA.at[x], at_x(k, c), gs)
    diags = Ds[...] + Dz[0] + Dz[1] + Dz[2]
    wait(gs)
    mixed = dec4(TA[:, :, 0:128].reshape(128, 128))
    side = dec4(TA[:, :, 128:256].reshape(128, 128))
    flip = mixed.T
    ga = jnp.where(ri == ci, diags[0:1], jnp.where(ri < ci, mixed, flip))
    gd = jnp.where(ri == ci, diags[1:2], jnp.where(ri > ci, mixed, flip))
    gram = jnp.concatenate(
        [jnp.concatenate([ga, side], axis=1), jnp.concatenate([side.T, gd], axis=1)], axis=0
    )
    hi = gram.astype(BF16)
    lo = (gram - hi.astype(F32)).astype(BF16)
    for h in (1, 0):
        cb = Cb[:, h * BLOCK:(h + 1) * BLOCK]
        through = nn(hi, cb) + nn(lo, cb)
        Ff[h] = (base[h] + through * (COV / (M - 1))).astype(BF16)
        if h == 1:
            fswap = put(Ff.at[1], Fo, partner)

    def part_a(k):
        at = pl.ds(pl.multiple_of(((x + k) % 4) * 64, 64), 64)
        part = nn(Ff[0, at, :], WT[0, :, 0:CUT]) + nn(Ff[1, at, :], WT[1, :, 0:CUT])
        return part.reshape(4, 16, CUT)

    part = (nn(Ff[0], WT[0, :, CUT:D_IN]) + nn(Ff[1], WT[1, :, CUT:D_IN])).reshape(4, 4, 16, REST)
    for j in range(4):
        B32[j] = part[:, j]
        Bc[j] = enc(part[:, j])
    bz = group()
    for k in (2, 1, 3):
        put(Bc.at[(zh + k) % 4], Bz.at[k - 1], at_z(k, c), bz)
    ps = group()
    for k in (2, 1, 3):
        Pc[k - 1] = enc(part_a(k))
        put(Pc.at[k - 1], Px.at[k - 1], at_x(k, c), ps)

    wait(fswap)
    for j in range(5):
        cols = pl.ds(j * 256, 256)
        L32[cols, :] = tn(X[:, :, cols].reshape(M, 256), Ff[0]) + tn(Xo[:, :, cols].reshape(M, 256), Fo[...])

    def rows_of(k, q):
        return pl.ds(pl.multiple_of(((y + k) % 4) * 320 + q * ROWS, ROWS), ROWS)

    sides = (pl.ds(0, 128), pl.ds(128, 128))
    ways = (1, 3)
    opp, direct, joint = {}, {}, {}
    for q in range(CHUNKS):
        opp[q], direct[q] = group(), group()
        for i in range(2):
            Lo[q, i] = enc(L32[rows_of(2, q), sides[i]])
            put(Lo.at[q, i], Ro.at[q, i], at_y(ways[i]), opp[q])

    def send_direct(q):
        for i in range(2):
            Ld[q, i] = enc(L32[rows_of(ways[i], q), sides[1 - i]])
            put(Ld.at[q, i], Rd.at[q, 1 - i], at_y(ways[i]), direct[q])

    send_direct(0)
    P0[...] = part_a(0)
    for q in range(CHUNKS):
        wait(opp[q])
        for i in range(2):
            Lc[q, i] = enc(L32[rows_of(ways[i], q), sides[i]] + dec(Ro[q, i]))
            put(Lc.at[q, i], Rc.at[q, i], at_y(ways[i]), direct[q])
        if q + 1 < CHUNKS:
            send_direct(q + 1)
    zz = []
    for q in range(CHUNKS):
        wait(direct[q])
        for i in range(2):
            Lz[q, i] = enc(L32[rows_of(0, q), sides[i]] + dec(Rd[q, i]) + dec(Rc[q, i]))
        zz.append(put(Lz.at[q], Lzr.at[q], across))

    wait(bz)
    for j in range(4):
        s = B32[zh, j] + dec(Bz[0, j]) + dec(Bz[1, j]) + dec(Bz[2, j])
        B2[j] = s
        Bx[j] = enc(s)
    bs = group()
    for k in (2, 1, 3):
        put(Bx.at[(x + k) % 4], Bxr.at[k - 1], at_x(k, c), bs)

    wait(ps)
    for j in range(4):
        s = P0[j] + dec(Px[0, j]) + dec(Px[1, j]) + dec(Px[2, j])
        S32[j] = s
        Pz[j] = enc(s)
    pz = group()
    for k in (2, 1, 3):
        put(Pz.at[(zh + k) % 4], Pzr.at[k - 1], at_z(k, c), pz)

    ls, kept = {}, []
    last = group()
    for q in range(CHUNKS):
        wait(zz[q])
        for i in range(2):
            La[q, :, sides[i]] = enc(dec(Lz[q, i]) + dec(Lzr[q, i]))
        here = lg.at[rows_of(0, q)]
        ls[q] = group()
        for way in ways:
            put(La.at[q], here, at_y(way), ls[q])
        kept.append(pltpu.make_async_copy(La.at[q], here, local.at[q]))
        kept[-1].start()

    for q in range(CHUNKS):
        wait(ls[q])
        for i in range(2):
            there = lg.at[rows_of(4 - ways[i], q), sides[i]]
            put(there, there, at_y(ways[i]), last)

    wait(pz)
    r = S32[zh] + dec(Pzr[0]) + dec(Pzr[1]) + dec(Pzr[2])
    R[:, :, 0:CUT] = r.reshape(2, 8, CUT)
    wait(bs)
    r = B2[x] + dec(Bxr[0]) + dec(Bxr[1]) + dec(Bxr[2])
    R[:, :, CUT:D_IN] = r.reshape(2, 8, REST)
    rswap = put(R.at[o], Rr, partner)
    wait(rswap)
    own, other = R[c], Rr[...]
    first = c == 0
    ig[:, 0, :] = jnp.where(first, own, other)
    ig[:, 1, :] = jnp.where(first, other, own)

    wait(last)
    for copy in kept:
        copy.wait()
    wait(sent)


def finish(ig, lg, image_grad, weight_grad, full, sem):
    copies = [pltpu.make_async_copy(ig, image_grad, sem.at[0])]
    copies[0].start()
    for j in range(5):
        at = pl.ds(j * 256, 256)
        full[at] = dec(lg[at])
        copies.append(pltpu.make_async_copy(full.at[at], weight_grad.at[at], sem.at[1 + j]))
        copies[-1].start()
    for copy in copies:
        copy.wait()


def shards(images, weight):
    V = pltpu.VMEM
    ig, lg = pl.pallas_call(
        kernel,
        out_shape=(
            jax.ShapeDtypeStruct((8, 2, D_IN), F32),
            jax.ShapeDtypeStruct((D_IN, BLOCK), BF16),
        ),
        in_specs=[pl.BlockSpec(memory_space=pltpu.HBM)] * 2,
        out_specs=[pl.BlockSpec(memory_space=V), pl.BlockSpec(memory_space=pl.ANY)],
        scratch_shapes=[
            V((8, 2, D_IN), BF16),
            V((D_IN, BLOCK), BF16),
            V((2, 8, D_IN), BF16),
            V((16, 16, D_IN), BF16),
            V((16, 16, D_IN), BF16),
            V((D_IN, BLOCK), BF16),
            V((2, BLOCK, D_IN), BF16),
            V((2, M, BLOCK), F32),
            V((M, 2 * BLOCK), BF16),
            V((2, M, BLOCK), F32),
            V((4, 32, 256), F32),
            V((4, 32, 256), BF16),
            V((3, 32, 256), BF16),
            V((32, 256), F32),
            V((32, 256), BF16),
            V((3, 32, 256), BF16),
            V((4, 32, 256), BF16),
            V((8, 128), F32),
            V((3, 8, 128), F32),
            V((8, 128), F32),
            V((3, 8, 128), F32),
            V((2, M, BLOCK), BF16),
            V((M, BLOCK), BF16),
            V((3, 4, 16, CUT), BF16),
            V((4, 16, CUT), F32),
            V((3, 4, 16, CUT), BF16),
            V((4, 16, CUT), F32),
            V((4, 16, CUT), BF16),
            V((3, 16, CUT), BF16),
            V((4, 4, 16, REST), F32),
            V((4, 4, 16, REST), BF16),
            V((3, 4, 16, REST), BF16),
            V((4, 16, REST), F32),
            V((4, 16, REST), BF16),
            V((3, 16, REST), BF16),
            V((2, 8, D_IN), F32),
            V((8, D_IN), F32),
            V((D_IN, BLOCK), F32),
            V((CHUNKS, 2, ROWS, 128), BF16),
            V((CHUNKS, 2, ROWS, 128), BF16),
            V((CHUNKS, 2, ROWS, 128), BF16),
            V((CHUNKS, 2, ROWS, 128), BF16),
            V((CHUNKS, 2, ROWS, 128), BF16),
            V((CHUNKS, 2, ROWS, 128), BF16),
            V((CHUNKS, 2, ROWS, 128), BF16),
            V((CHUNKS, 2, ROWS, 128), BF16),
            V((CHUNKS, ROWS, BLOCK), BF16),
            V((10240, 128), F32),
            pltpu.SemaphoreType.DMA,
            pltpu.SemaphoreType.DMA((NGROUPS,)),
            pltpu.SemaphoreType.DMA((4,)),
        ],
        compiler_params=pltpu.CompilerParams(
            collective_id=0, has_side_effects=True, vmem_limit_bytes=VLIM
        ),
    )(pltpu.with_memory_space_constraint(images, pltpu.HBM), pltpu.with_memory_space_constraint(weight, pltpu.HBM))
    return pl.pallas_call(
        finish,
        out_shape=(
            jax.ShapeDtypeStruct((8, 2, D_IN), F32),
            jax.ShapeDtypeStruct((D_IN, BLOCK), F32),
        ),
        in_specs=[pl.BlockSpec(memory_space=V)] * 2,
        out_specs=[pl.BlockSpec(memory_space=pl.ANY)] * 2,
        scratch_shapes=[V((D_IN, BLOCK), F32), pltpu.SemaphoreType.DMA((6,))],
        compiler_params=pltpu.CompilerParams(vmem_limit_bytes=4 * 2**20),
    )(ig, lg)


NGROUPS = 40
VLIM = 24 * 2**20


def solution(mesh):
    return jax.shard_map(
        shards,
        mesh=mesh,
        in_specs=(P(("rep", "dp"), None, None), P(None, "dp")),
        out_specs=(P(("rep", "dp"), None, None), P(None, "dp")),
        check_vma=False,
    )
```

time: 63.1 us -> 57.8 us (0.916)
  local copies, waits for them, and re-layouts: 2.49 us -> 0 us
  other arithmetic: 1.57 us -> 0 us
  Pallas kernels: 58.2 us -> 56.8 us
    pallas_call x1, Pallas kernels: 58.2 us -> 55.5 us  [shards(): pl.pallas_call(kernel, out_shape=(jax.ShapeDtypeStruct((8, 2, D_IN), F32)...]
    unnamed x5 -> x0, local copies, waits for them, and re-layouts: 2.49 us -> none
    select_n x1 -> x0, other arithmetic: 1.57 us -> none  [dec(): return jnp.where(t < 0.0, -s, s)]
    pallas_call x0 -> x1, Pallas kernels: none -> 1.27 us  [shards(): pl.pallas_call(finish, out_shape=(jax.ShapeDtypeStruct((8, 2, D_IN), F32)...]
where the time goes in v3:
time: 57.8 us; the launch traced here: 57.4 us
  Pallas kernels  56.8 us (98%)
  between operations  0.64 us (1%)
    pallas_call x1, Pallas kernels, shards(): pl.pallas_call(kernel, out_shape=(jax.ShapeDtypeStruct((8, 2, D_IN), F32)...  55.5 us
    pallas_call x1, Pallas kernels, shards(): pl.pallas_call(finish, out_shape=(jax.ShapeDtypeStruct((8, 2, D_IN), F32)...  1.27 us

profile of v3, /device:TPU:8, one launch (start us, length us, event | category | flops | bytes accessed | tf_op | source)
XLA Modules:
  0.0 57.4 jit_solution(6764712177845037424)
XLA Ops:
  0.6 55.5 %shard_map.41 = (f32[8,2,1280]{2,1,0:T(2,128)S(1)}, bf16[1280,256]{1,0:T(8,128)(2,1)S(1)}) custom-call(bf16[8,2,1280]{2,1,0:T(2,128)(2,1)} %img.1, bf16[1280,256]{1,0:T(8,128)(2,1)} %w_hbm.1), custom_call_target="tpu_custom_call" | custom-call | tf_op jit(solution)/shard_map/pallas_call | solution.py:364
  56.2 1.3 %shard_map.42 = (f32[8,2,1280]{2,1,0:T(2,128)}, f32[1280,256]{1,0:T(8,128)}) custom-call(f32[8,2,1280]{2,1,0:T(2,128)S(1)} %get-tuple-element.4.ig, bf16[1280,256]{1,0:T(8,128)(2,1)S(1)} %get-tuple-element.5.lg), custom_call_target="tpu_custom_call" | custom-call | tf_op jit(solution)/shard_map/pallas_call | solution.py:429

commit v4 on v3

--- a/solution.py
+++ b/solution.py
@@ -69,11 +69,11 @@
 
 def kernel(
     img, w_hbm, ig, lg,
-    Iv, w, I2, X, Xo, Wo, WT, E, Cb, base,
-    T, Tc, Tx, Sz, Sc, Szr, TA, Dg, Dx, Ds, Dz,
-    Ff, Fo,
-    Pc, P0, Px, S32, Pz, Pzr,
-    B32, Bc, Bz, B2, Bx, Bxr, R, Rr,
+    Iv, w, I2, X, Xo, XT, Wo, WT, E, Cb, Cbo, base,
+    T, Tc, Tx, Sz, Sc, Szr, TA, Dg, Dx, Ds, Dz, Dt,
+    Ff,
+    P32, Pc, Px, S32, Pz, Pzr, So,
+    B32, Bc, Bz, B2, Bx, Bxr, Bo,
     L32, Lo, Ld, Lc, Ro, Rd, Rc, Lz, Lzr, La,
     span, send, recv, local,
 ):
@@ -200,63 +200,55 @@
         put(Sc, Szr.at[k - 1], at_z(k, c), ss)
         put(Ds, Dz.at[k - 1], at_z(k, c), ss)
 
+    def ungrammed(e, gap, cb):
+        centred = e - jnp.mean(e, axis=0, keepdims=True)
+        spread = jnp.sqrt(jnp.sum(centred * centred, axis=0, keepdims=True) / (M - 1) + EPS)
+        pull = jnp.where(spread < 1.0, -VAR / spread, 0.0)
+        diag = jnp.sum(cb * cb, axis=0, keepdims=True) / (M - 1)
+        return INV * gap + pull * centred - (COV * diag) * cb
+
     wait(xswap)
     orows = Xo[...].reshape(M, D_IN)
     for h, wr in enumerate((w, Wo)):
-        e = E[h]
-        gap = e - nn(orows, wr[...])
-        centred = e - jnp.mean(e, axis=0, keepdims=True)
-        spread = jnp.sqrt(jnp.sum(centred * centred, axis=0, keepdims=True) / (M - 1) + EPS)
-        pull = jnp.where(spread < 1.0, -VAR / spread, 0.0)
+        e, eo = E[h], nn(orows, wr[...])
         cb = Cb[:, h * BLOCK:(h + 1) * BLOCK].astype(F32)
-        diag = jnp.sum(cb * cb, axis=0, keepdims=True) / (M - 1)
-        base[h] = INV * gap + pull * centred - (COV * diag) * cb
+        base[h] = ungrammed(e, e - eo, cb)
+        if h == 0:
+            cb = (eo - jnp.mean(eo, axis=0, keepdims=True)).astype(BF16)
+            Cbo[...] = cb
+            base[2] = ungrammed(eo, eo - e, cb.astype(F32))
+    XT[0] = rows.T
+    XT[1] = orows.T
 
     wait(ss)
-    TA[x] = enc4(Sz[...] + dec4(Szr[0]) + dec4(Szr[1]) + dec4(Szr[2]))
+    TA[c, x] = enc4(Sz[...] + dec4(Szr[0]) + dec4(Szr[1]) + dec4(Szr[2]))
     gs = group()
     for k in (2, 1, 3):
-        put(TA.at[x], TA.at[x], at_x(k, c), gs)
-    diags = Ds[...] + Dz[0] + Dz[1] + Dz[2]
+        for core in (c, o):
+            put(TA.at[c, x], TA.at[c, x], at_x(k, core), gs)
+    put(TA.at[c, x], TA.at[c, x], partner, gs)
+    Dt[c] = Ds[...] + Dz[0] + Dz[1] + Dz[2]
+    put(Dt.at[c], Dt.at[c], partner, gs)
     wait(gs)
-    mixed = dec4(TA[:, :, 0:128].reshape(128, 128))
-    side = dec4(TA[:, :, 128:256].reshape(128, 128))
-    flip = mixed.T
-    ga = jnp.where(ri == ci, diags[0:1], jnp.where(ri < ci, mixed, flip))
-    gd = jnp.where(ri == ci, diags[1:2], jnp.where(ri > ci, mixed, flip))
-    gram = jnp.concatenate(
-        [jnp.concatenate([ga, side], axis=1), jnp.concatenate([side.T, gd], axis=1)], axis=0
-    )
-    hi = gram.astype(BF16)
-    lo = (gram - hi.astype(F32)).astype(BF16)
-    for h in (1, 0):
-        cb = Cb[:, h * BLOCK:(h + 1) * BLOCK]
-        through = nn(hi, cb) + nn(lo, cb)
-        Ff[h] = (base[h] + through * (COV / (M - 1))).astype(BF16)
-        if h == 1:
-            fswap = put(Ff.at[1], Fo, partner)
-
-    def part_a(k):
-        at = pl.ds(pl.multiple_of(((x + k) % 4) * 64, 64), 64)
-        part = nn(Ff[0, at, :], WT[0, :, 0:CUT]) + nn(Ff[1, at, :], WT[1, :, 0:CUT])
-        return part.reshape(4, 16, CUT)
-
-    part = (nn(Ff[0], WT[0, :, CUT:D_IN]) + nn(Ff[1], WT[1, :, CUT:D_IN])).reshape(4, 4, 16, REST)
-    for j in range(4):
-        B32[j] = part[:, j]
-        Bc[j] = enc(part[:, j])
-    bz = group()
-    for k in (2, 1, 3):
-        put(Bc.at[(zh + k) % 4], Bz.at[k - 1], at_z(k, c), bz)
-    ps = group()
-    for k in (2, 1, 3):
-        Pc[k - 1] = enc(part_a(k))
-        put(Pc.at[k - 1], Px.at[k - 1], at_x(k, c), ps)
-
-    wait(fswap)
-    for j in range(5):
-        cols = pl.ds(j * 256, 256)
-        L32[cols, :] = tn(X[:, :, cols].reshape(M, 256), Ff[0]) + tn(Xo[:, :, cols].reshape(M, 256), Fo[...])
+    def gram_of(view):
+        mixed = dec4(TA[view, :, :, 0:128].reshape(128, 128))
+        side = dec4(TA[view, :, :, 128:256].reshape(128, 128))
+        flip = mixed.T
+        ga = jnp.where(ri == ci, Dt[view, 0:1], jnp.where(ri < ci, mixed, flip))
+        gd = jnp.where(ri == ci, Dt[view, 1:2], jnp.where(ri > ci, mixed, flip))
+        gram = jnp.concatenate(
+            [jnp.concatenate([ga, side], axis=1), jnp.concatenate([side.T, gd], axis=1)], axis=0
+        )
+        hi = gram.astype(BF16)
+        return hi, (gram - hi.astype(F32)).astype(BF16)
+
+    def feature_grad(gram, cb, rest):
+        through = nn(gram[0], cb) + nn(gram[1], cb)
+        return (rest + through * (COV / (M - 1))).astype(BF16)
+
+    gram = gram_of(c)
+    Ff[0] = feature_grad(gram, Cb[:, 0:BLOCK], base[0])
+    L32[...] = nn(XT[0], Ff[0]) + nn(XT[1], feature_grad(gram_of(o), Cbo[...], base[2]))
 
     def rows_of(k, q):
         return pl.ds(pl.multiple_of(((y + k) % 4) * 320 + q * ROWS, ROWS), ROWS)
@@ -276,7 +268,23 @@
             put(Ld.at[q, i], Rd.at[q, 1 - i], at_y(ways[i]), direct[q])
 
     send_direct(0)
-    P0[...] = part_a(0)
+    Ff[1] = feature_grad(gram, Cb[:, BLOCK:2 * BLOCK], base[1])
+    part = nn(Ff[0], WT[0]) + nn(Ff[1], WT[1])
+    P32[...] = part[:, 0:CUT].reshape(4, 4, 16, CUT)
+    part = part[:, CUT:D_IN].reshape(4, 4, 16, REST)
+    halves = (pl.ds(0, CUT // 2), pl.ds(CUT // 2, CUT // 2))
+    Pc[...] = enc(P32[...])
+    for j in range(4):
+        B32[j] = part[:, j]
+        Bc[j] = enc(part[:, j])
+    ps = [group(), group()]
+    bz = group()
+    for i in range(2):
+        for k in (2, 1, 3):
+            put(Pc.at[(x + k) % 4, :, :, halves[i]], Px.at[k - 1, :, :, halves[i]], at_x(k, c), ps[i])
+        if i == 0:
+            for k in (2, 1, 3):
+                put(Bc.at[(zh + k) % 4], Bz.at[k - 1], at_z(k, c), bz)
     for q in range(CHUNKS):
         wait(opp[q])
         for i in range(2):
@@ -284,59 +292,89 @@
             put(Lc.at[q, i], Rc.at[q, i], at_y(ways[i]), direct[q])
         if q + 1 < CHUNKS:
             send_direct(q + 1)
-    zz = []
-    for q in range(CHUNKS):
+
+    def at_core(core):
+        return pl.ds(pl.multiple_of(core * 8, 8), 8)
+
+    mates = group()
+
+    def sum_a(i):
+        wait(ps[i])
+        cols = halves[i]
+        for j in range(4):
+            s = P32[x, j, :, cols] + dec(Px[0, j, :, cols]) + dec(Px[1, j, :, cols]) + dec(Px[2, j, :, cols])
+            S32[j, :, cols] = s
+            Pz[j, :, cols] = enc(s)
+        at = group()
+        for k in (2, 1, 3):
+            for core in (c, o):
+                put(Pz.at[(zh + k) % 4, at_core(core), cols], Pzr.at[k - 1, c, :, cols], at_z(k, core), at)
+        put(S32.at[zh, at_core(o), cols], So.at[:, cols], partner, mates)
+        return at
+
+    def sum_b():
+        wait(bz)
+        for j in range(4):
+            s = B32[zh, j] + dec(Bz[0, j]) + dec(Bz[1, j]) + dec(Bz[2, j])
+            B2[j] = s
+            Bx[j] = enc(s)
+        at = group()
+        for k in (2, 1, 3):
+            for core in (c, o):
+                put(Bx.at[(x + k) % 4, at_core(core)], Bxr.at[k - 1, c], at_x(k, core), at)
+        put(B2.at[x, at_core(o)], Bo, partner, mates)
+        return at
+
+    zz, ls, kept = {}, {}, []
+    last = group()
+
+    def sum_l(q):
         wait(direct[q])
         for i in range(2):
             Lz[q, i] = enc(L32[rows_of(0, q), sides[i]] + dec(Rd[q, i]) + dec(Rc[q, i]))
-        zz.append(put(Lz.at[q], Lzr.at[q], across))
-
-    wait(bz)
-    for j in range(4):
-        s = B32[zh, j] + dec(Bz[0, j]) + dec(Bz[1, j]) + dec(Bz[2, j])
-        B2[j] = s
-        Bx[j] = enc(s)
-    bs = group()
-    for k in (2, 1, 3):
-        put(Bx.at[(x + k) % 4], Bxr.at[k - 1], at_x(k, c), bs)
-
-    wait(ps)
-    for j in range(4):
-        s = P0[j] + dec(Px[0, j]) + dec(Px[1, j]) + dec(Px[2, j])
-        S32[j] = s
-        Pz[j] = enc(s)
-    pz = group()
-    for k in (2, 1, 3):
-        put(Pz.at[(zh + k) % 4], Pzr.at[k - 1], at_z(k, c), pz)
-
-    ls, kept = {}, []
-    last = group()
-    for q in range(CHUNKS):
+        zz[q] = put(Lz.at[q], Lzr.at[q], across)
+
+    def share_l(q):
         wait(zz[q])
         for i in range(2):
             La[q, :, sides[i]] = enc(dec(Lz[q, i]) + dec(Lzr[q, i]))
         here = lg.at[rows_of(0, q)]
-        ls[q] = group()
-        for way in ways:
-            put(La.at[q], here, at_y(way), ls[q])
+        for k in (2, 1, 3):
+            put(La.at[q], here, at_y(k), last)
         kept.append(pltpu.make_async_copy(La.at[q], here, local.at[q]))
         kept[-1].start()
 
-    for q in range(CHUNKS):
-        wait(ls[q])
-        for i in range(2):
-            there = lg.at[rows_of(4 - ways[i], q), sides[i]]
-            put(there, there, at_y(ways[i]), last)
-
-    wait(pz)
-    r = S32[zh] + dec(Pzr[0]) + dec(Pzr[1]) + dec(Pzr[2])
-    R[:, :, 0:CUT] = r.reshape(2, 8, CUT)
+    def forward_l(q):
+        pass
+
+    pz = []
+    sum_l(0)
+    sum_l(1)
+    sum_l(2)
+    share_l(0)
+    sum_l(3)
+    share_l(1)
+    pz.append(sum_a(0))
+    bs = sum_b()
+    pz.append(sum_a(1))
+    share_l(2)
+    share_l(3)
+
+    wait(mates)
+    mine = at_core(c)
+
+    def total(view, first, second):
+        a, b = first, second
+        for k in range(3):
+            a = a + dec(Pzr[k, view])
+            b = b + dec(Bxr[k, view])
+        return jnp.concatenate([a, b], axis=1)
+
+    wait(pz[0])
+    wait(pz[1])
     wait(bs)
-    r = B2[x] + dec(Bxr[0]) + dec(Bxr[1]) + dec(Bxr[2])
-    R[:, :, CUT:D_IN] = r.reshape(2, 8, REST)
-    rswap = put(R.at[o], Rr, partner)
-    wait(rswap)
-    own, other = R[c], Rr[...]
+    own = total(c, S32[zh, mine], B2[x, mine])
+    other = total(o, So[...], Bo[...])
     first = c == 0
     ig[:, 0, :] = jnp.where(first, own, other)
     ig[:, 1, :] = jnp.where(first, other, own)
@@ -375,38 +413,40 @@
             V((2, 8, D_IN), BF16),
             V((16, 16, D_IN), BF16),
             V((16, 16, D_IN), BF16),
+            V((2, D_IN, M), BF16),
             V((D_IN, BLOCK), BF16),
             V((2, BLOCK, D_IN), BF16),
             V((2, M, BLOCK), F32),
             V((M, 2 * BLOCK), BF16),
-            V((2, M, BLOCK), F32),
+            V((M, BLOCK), BF16),
+            V((3, M, BLOCK), F32),
             V((4, 32, 256), F32),
             V((4, 32, 256), BF16),
             V((3, 32, 256), BF16),
             V((32, 256), F32),
             V((32, 256), BF16),
             V((3, 32, 256), BF16),
-            V((4, 32, 256), BF16),
+            V((2, 4, 32, 256), BF16),
             V((8, 128), F32),
             V((3, 8, 128), F32),
             V((8, 128), F32),
             V((3, 8, 128), F32),
+            V((2, 8, 128), F32),
             V((2, M, BLOCK), BF16),
-            V((M, BLOCK), BF16),
-            V((3, 4, 16, CUT), BF16),
-            V((4, 16, CUT), F32),
+            V((4, 4, 16, CUT), F32),
+            V((4, 4, 16, CUT), BF16),
             V((3, 4, 16, CUT), BF16),
             V((4, 16, CUT), F32),
             V((4, 16, CUT), BF16),
-            V((3, 16, CUT), BF16),
+            V((3, 2, 8, CUT), BF16),
+            V((8, CUT), F32),
             V((4, 4, 16, REST), F32),
             V((4, 4, 16, REST), BF16),
             V((3, 4, 16, REST), BF16),
             V((4, 16, REST), F32),
             V((4, 16, REST), BF16),
-            V((3, 16, REST), BF16),
-            V((2, 8, D_IN), F32),
-            V((8, D_IN), F32),
+            V((3, 2, 8, REST), BF16),
+            V((8, REST), F32),
             V((D_IN, BLOCK), F32),
             V((CHUNKS, 2, ROWS, 128), BF16),
             V((CHUNKS, 2, ROWS, 128), BF16),

time: 57.8 us -> 55.6 us (0.962)
  Pallas kernels: 56.8 us -> 54.8 us
    pallas_call x1, Pallas kernels: 55.5 us -> 53.6 us  [shards(): pl.pallas_call(kernel, out_shape=(jax.ShapeDtypeStruct((8, 2, D_IN), F32)...]
where the time goes in v4:
time: 55.6 us; the launch traced here: 55.5 us
  Pallas kernels  54.8 us (99%)
  between operations  0.64 us (1%)
    pallas_call x1, Pallas kernels, shards(): pl.pallas_call(kernel, out_shape=(jax.ShapeDtypeStruct((8, 2, D_IN), F32)...  53.6 us
    pallas_call x1, Pallas kernels, shards(): pl.pallas_call(finish, out_shape=(jax.ShapeDtypeStruct((8, 2, D_IN), F32)...  1.27 us

profile of v4, /device:TPU:8, one launch (start us, length us, event | category | flops | bytes accessed | tf_op | source)
XLA Modules:
  0.0 55.5 jit_solution(1229725001393993088)
XLA Ops:
  0.6 53.6 %shard_map.41 = (f32[8,2,1280]{2,1,0:T(2,128)S(1)}, bf16[1280,256]{1,0:T(8,128)(2,1)S(1)}) custom-call(bf16[8,2,1280]{2,1,0:T(2,128)(2,1)} %img.1, bf16[1280,256]{1,0:T(8,128)(2,1)} %w_hbm.1), custom_call_target="tpu_custom_call" | custom-call | tf_op jit(solution)/shard_map/pallas_call | solution.py:402
  54.2 1.3 %shard_map.42 = (f32[8,2,1280]{2,1,0:T(2,128)}, f32[1280,256]{1,0:T(8,128)}) custom-call(f32[8,2,1280]{2,1,0:T(2,128)S(1)} %get-tuple-element.4.ig, bf16[1280,256]{1,0:T(8,128)(2,1)S(1)} %get-tuple-element.5.lg), custom_call_target="tpu_custom_call" | custom-call | tf_op jit(solution)/shard_map/pallas_call | solution.py:469

commit v5 on v4

--- a/solution.py
+++ b/solution.py
@@ -22,6 +22,8 @@
 ROWS = D_IN // 4 // CHUNKS
 CUT = 1024
 REST = D_IN - CUT
+PCUT = 1024
+PREST = D_IN - PCUT
 GRAM_UNIT = 2.0**-10
 
 
@@ -74,8 +76,8 @@
     Ff,
     P32, Pc, Px, S32, Pz, Pzr, So,
     B32, Bc, Bz, B2, Bx, Bxr, Bo,
-    L32, Lo, Ld, Lc, Ro, Rd, Rc, Lz, Lzr, La,
-    span, send, recv, local,
+    L32, Ly, Lr, Lz, Lzr, La,
+    span, send, recv, local, near,
 ):
     rep, dp = lax.axis_index("rep"), lax.axis_index("dp")
     y, zl = rep // 2, rep % 2
@@ -103,7 +105,9 @@
     barrier = pltpu.get_barrier_semaphore()
     peers = [partner, across]
     for k in (1, 2, 3):
-        peers += [at_x(k, c), at_z(k, c), at_x(k, o), at_z(k, o), at_y(k)]
+        peers += [at_x(k, c), at_x(k, o), at_y(k)]
+    for k in (1, 3):
+        peers += [at_z(k, c), at_z(k, o)]
     for peer in peers:
         pl.semaphore_signal(barrier, inc=1, device_id=peer, device_id_type=MESH)
     fetch.wait()
@@ -111,6 +115,7 @@
     I2[0] = both[:, 0, :].astype(BF16)
     I2[1] = both[:, 1, :].astype(BF16)
     pl.semaphore_wait(barrier, len(peers))
+    pl.semaphore_signal(near, inc=1, device_id=at_z(1, c), device_id_type=MESH)
 
     sent = Group(send)
     groups = []
@@ -144,7 +149,8 @@
     for k in (1, 3, 2):
         az[k], bx[k] = group(), group()
         for core in (c, o):
-            put(I2.at[core, :, A], X.at[chip, at, A], at_z(k, core), az[k])
+            if k != 2:
+                put(I2.at[core, :, A], X.at[chip, at, A], at_z(k, core), az[k])
             put(I2.at[core, :, B], X.at[chip, at, B], at_x(k, core), bx[k])
     mate = put(I2.at[o], X.at[chip, at], partner)
     keep = pltpu.make_async_copy(I2.at[c], X.at[chip, at], local.at[0])
@@ -153,6 +159,9 @@
     keep.wait()
     wait(mate)
     forwards = group()
+    pl.semaphore_wait(near, 1)
+    for core in (c, o):
+        put(I2.at[core, :, A], X.at[chip, at, A], at_z(2, core), az[2])
     for k in (0, 1, 3, 2):
         if k:
             wait(az[k])
@@ -222,13 +231,13 @@
 
     wait(ss)
     TA[c, x] = enc4(Sz[...] + dec4(Szr[0]) + dec4(Szr[1]) + dec4(Szr[2]))
-    gs = group()
-    for k in (2, 1, 3):
-        for core in (c, o):
-            put(TA.at[c, x], TA.at[c, x], at_x(k, core), gs)
-    put(TA.at[c, x], TA.at[c, x], partner, gs)
+    gs, go = group(), group()
+    for core, at in ((c, gs), (o, go)):
+        for k in (2, 1, 3):
+            put(TA.at[c, x], TA.at[c, x], at_x(k, core), at)
+    put(TA.at[c, x], TA.at[c, x], partner, go)
     Dt[c] = Ds[...] + Dz[0] + Dz[1] + Dz[2]
-    put(Dt.at[c], Dt.at[c], partner, gs)
+    put(Dt.at[c], Dt.at[c], partner, go)
     wait(gs)
     def gram_of(view):
         mixed = dec4(TA[view, :, :, 0:128].reshape(128, 128))
@@ -248,35 +257,31 @@
 
     gram = gram_of(c)
     Ff[0] = feature_grad(gram, Cb[:, 0:BLOCK], base[0])
-    L32[...] = nn(XT[0], Ff[0]) + nn(XT[1], feature_grad(gram_of(o), Cbo[...], base[2]))
-
-    def rows_of(k, q):
-        return pl.ds(pl.multiple_of(((y + k) % 4) * 320 + q * ROWS, ROWS), ROWS)
-
-    sides = (pl.ds(0, 128), pl.ds(128, 128))
-    ways = (1, 3)
-    opp, direct, joint = {}, {}, {}
-    for q in range(CHUNKS):
-        opp[q], direct[q] = group(), group()
-        for i in range(2):
-            Lo[q, i] = enc(L32[rows_of(2, q), sides[i]])
-            put(Lo.at[q, i], Ro.at[q, i], at_y(ways[i]), opp[q])
-
-    def send_direct(q):
-        for i in range(2):
-            Ld[q, i] = enc(L32[rows_of(ways[i], q), sides[1 - i]])
-            put(Ld.at[q, i], Rd.at[q, 1 - i], at_y(ways[i]), direct[q])
-
-    send_direct(0)
     Ff[1] = feature_grad(gram, Cb[:, BLOCK:2 * BLOCK], base[1])
     part = nn(Ff[0], WT[0]) + nn(Ff[1], WT[1])
-    P32[...] = part[:, 0:CUT].reshape(4, 4, 16, CUT)
-    part = part[:, CUT:D_IN].reshape(4, 4, 16, REST)
-    halves = (pl.ds(0, CUT // 2), pl.ds(CUT // 2, CUT // 2))
+    P32[...] = part[:, 0:PCUT].reshape(4, 4, 16, PCUT)
+    part = part[:, PCUT:D_IN].reshape(4, 4, 16, PREST)
+    halves = (pl.ds(0, PCUT // 2), pl.ds(PCUT // 2, PCUT // 2))
     Pc[...] = enc(P32[...])
     for j in range(4):
         B32[j] = part[:, j]
         Bc[j] = enc(part[:, j])
+    L32[...] = nn(XT[0], Ff[0])
+
+    wait(go)
+    L32[...] += nn(XT[1], feature_grad(gram_of(o), Cbo[...], base[2]))
+
+    def rows_of(k, q):
+        return pl.ds(pl.multiple_of(((y + k) % 4) * 320 + q * ROWS, ROWS), ROWS)
+
+    sides = (pl.ds(0, 128), pl.ds(128, 128))
+    direct = {}
+    for q in range(CHUNKS):
+        direct[q] = group()
+        for k in (2, 1, 3):
+            for i in range(2):
+                Ly[q, k - 1, i] = enc(L32[rows_of(k, q), sides[i]])
+            put(Ly.at[q, k - 1], Lr.at[q, k - 1], at_y(k), direct[q])
     ps = [group(), group()]
     bz = group()
     for i in range(2):
@@ -285,14 +290,6 @@
         if i == 0:
             for k in (2, 1, 3):
                 put(Bc.at[(zh + k) % 4], Bz.at[k - 1], at_z(k, c), bz)
-    for q in range(CHUNKS):
-        wait(opp[q])
-        for i in range(2):
-            Lc[q, i] = enc(L32[rows_of(ways[i], q), sides[i]] + dec(Ro[q, i]))
-            put(Lc.at[q, i], Rc.at[q, i], at_y(ways[i]), direct[q])
-        if q + 1 < CHUNKS:
-            send_direct(q + 1)
-
     def at_core(core):
         return pl.ds(pl.multiple_of(core * 8, 8), 8)
 
@@ -325,13 +322,13 @@
         put(B2.at[x, at_core(o)], Bo, partner, mates)
         return at
 
-    zz, ls, kept = {}, {}, []
+    zz, kept = {}, []
     last = group()
 
     def sum_l(q):
         wait(direct[q])
         for i in range(2):
-            Lz[q, i] = enc(L32[rows_of(0, q), sides[i]] + dec(Rd[q, i]) + dec(Rc[q, i]))
+            Lz[q, i] = enc(L32[rows_of(0, q), sides[i]] + dec(Lr[q, 0, i]) + dec(Lr[q, 1, i]) + dec(Lr[q, 2, i]))
         zz[q] = put(Lz.at[q], Lzr.at[q], across)
 
     def share_l(q):
@@ -344,19 +341,16 @@
         kept.append(pltpu.make_async_copy(La.at[q], here, local.at[q]))
         kept[-1].start()
 
-    def forward_l(q):
-        pass
-
     pz = []
     sum_l(0)
     sum_l(1)
-    sum_l(2)
-    share_l(0)
-    sum_l(3)
-    share_l(1)
     pz.append(sum_a(0))
     bs = sum_b()
+    share_l(0)
+    sum_l(2)
     pz.append(sum_a(1))
+    share_l(1)
+    sum_l(3)
     share_l(2)
     share_l(3)
 
@@ -433,27 +427,23 @@
             V((3, 8, 128), F32),
             V((2, 8, 128), F32),
             V((2, M, BLOCK), BF16),
-            V((4, 4, 16, CUT), F32),
-            V((4, 4, 16, CUT), BF16),
-            V((3, 4, 16, CUT), BF16),
-            V((4, 16, CUT), F32),
-            V((4, 16, CUT), BF16),
-            V((3, 2, 8, CUT), BF16),
-            V((8, CUT), F32),
-            V((4, 4, 16, REST), F32),
-            V((4, 4, 16, REST), BF16),
-            V((3, 4, 16, REST), BF16),
-            V((4, 16, REST), F32),
-            V((4, 16, REST), BF16),
-            V((3, 2, 8, REST), BF16),
-            V((8, REST), F32),
+            V((4, 4, 16, PCUT), F32),
+            V((4, 4, 16, PCUT), BF16),
+            V((3, 4, 16, PCUT), BF16),
+            V((4, 16, PCUT), F32),
+            V((4, 16, PCUT), BF16),
+            V((3, 2, 8, PCUT), BF16),
+            V((8, PCUT), F32),
+            V((4, 4, 16, PREST), F32),
+            V((4, 4, 16, PREST), BF16),
+            V((3, 4, 16, PREST), BF16),
+            V((4, 16, PREST), F32),
+            V((4, 16, PREST), BF16),
+            V((3, 2, 8, PREST), BF16),
+            V((8, PREST), F32),
             V((D_IN, BLOCK), F32),
-            V((CHUNKS, 2, ROWS, 128), BF16),
-            V((CHUNKS, 2, ROWS, 128), BF16),
-            V((CHUNKS, 2, ROWS, 128), BF16),
-            V((CHUNKS, 2, ROWS, 128), BF16),
-            V((CHUNKS, 2, ROWS, 128), BF16),
-            V((CHUNKS, 2, ROWS, 128), BF16),
+            V((CHUNKS, 3, 2, ROWS, 128), BF16),
+            V((CHUNKS, 3, 2, ROWS, 128), BF16),
             V((CHUNKS, 2, ROWS, 128), BF16),
             V((CHUNKS, 2, ROWS, 128), BF16),
             V((CHUNKS, ROWS, BLOCK), BF16),
@@ -461,6 +451,7 @@
             pltpu.SemaphoreType.DMA,
             pltpu.SemaphoreType.DMA((NGROUPS,)),
             pltpu.SemaphoreType.DMA((4,)),
+            pltpu.SemaphoreType.REGULAR,
         ],
         compiler_params=pltpu.CompilerParams(
             collective_id=0, has_side_effects=True, vmem_limit_bytes=VLIM

time: 55.6 us -> 54.3 us (0.977)
  Pallas kernels: 54.8 us -> 53.5 us
    pallas_call x1, Pallas kernels: 53.6 us -> 52.3 us  [shards(): pl.pallas_call(kernel, out_shape=(jax.ShapeDtypeStruct((8, 2, D_IN), F32)...]
where the time goes in v5:
time: 54.3 us; the launch traced here: 54.2 us
  Pallas kernels  53.5 us (99%)
  between operations  0.64 us (1%)
    pallas_call x1, Pallas kernels, shards(): pl.pallas_call(kernel, out_shape=(jax.ShapeDtypeStruct((8, 2, D_IN), F32)...  52.3 us
    pallas_call x1, Pallas kernels, shards(): pl.pallas_call(finish, out_shape=(jax.ShapeDtypeStruct((8, 2, D_IN), F32)...  1.27 us

profile of v5, /device:TPU:8, one launch (start us, length us, event | category | flops | bytes accessed | tf_op | source)
XLA Modules:
  0.0 54.2 jit_solution(18032199601599795877)
XLA Ops:
  0.6 52.3 %shard_map.41 = (f32[8,2,1280]{2,1,0:T(2,128)S(1)}, bf16[1280,256]{1,0:T(8,128)(2,1)S(1)}) custom-call(bf16[8,2,1280]{2,1,0:T(2,128)(2,1)} %img.1, bf16[1280,256]{1,0:T(8,128)(2,1)} %w_hbm.1), custom_call_target="tpu_custom_call" | custom-call | tf_op jit(solution)/shard_map/pallas_call | solution.py:396
  52.9 1.3 %shard_map.42 = (f32[8,2,1280]{2,1,0:T(2,128)}, f32[1280,256]{1,0:T(8,128)}) custom-call(f32[8,2,1280]{2,1,0:T(2,128)S(1)} %get-tuple-element.4.ig, bf16[1280,256]{1,0:T(8,128)(2,1)S(1)} %get-tuple-element.5.lg), custom_call_target="tpu_custom_call" | custom-call | tf_op jit(solution)/shard_map/pallas_call | solution.py:460

commit v6 on v5

--- a/solution.py
+++ b/solution.py
@@ -18,9 +18,10 @@
 INV = S * 2.0 * 25.0 / (M * EMB)
 VAR = S * 25.0 / (EMB * (M - 1))
 COV = S * 4.0 / (EMB * (M - 1))
-CHUNKS = 4
-ROWS = D_IN // 4 // CHUNKS
-CUT = 1024
+PIECE = D_IN // 4
+SIZES = (64, 96, 96, 64)
+CHUNKS = len(SIZES)
+CUT = 896
 REST = D_IN - CUT
 PCUT = 1024
 PREST = D_IN - PCUT
@@ -162,17 +163,19 @@
     pl.semaphore_wait(near, 1)
     for core in (c, o):
         put(I2.at[core, :, A], X.at[chip, at, A], at_z(2, core), az[2])
-    for k in (0, 1, 3, 2):
-        if k:
-            wait(az[k])
-        slot = x * 4 + (zh - k + 4) % 4
-        for j in (2, 1, 3):
-            put(X.at[slot, :, A], X.at[slot, :, A], at_x(j, c), forwards)
-        if k:
-            wait(bx[k])
-        slot = ((x - k + 4) % 4) * 4 + zh
-        for j in (2, 1, 3):
-            put(X.at[slot, :, B], X.at[slot, :, B], at_z(j, c), forwards)
+    for name, k in (("A", 0), ("B", 0), ("B", 1), ("B", 3), ("A", 1), ("A", 3), ("B", 2), ("A", 2)):
+        if name == "A":
+            if k:
+                wait(az[k])
+            slot = x * 4 + (zh - k + 4) % 4
+            for j in (2, 1, 3):
+                put(X.at[slot, :, A], X.at[slot, :, A], at_x(j, c), forwards)
+        else:
+            if k:
+                wait(bx[k])
+            slot = ((x - k + 4) % 4) * 4 + zh
+            for j in (2, 1, 3):
+                put(X.at[slot, :, B], X.at[slot, :, B], at_z(j, c), forwards)
     wait(wswap)
     wfetch.wait()
     WT[0] = w[...].T
@@ -271,17 +274,18 @@
     wait(go)
     L32[...] += nn(XT[1], feature_grad(gram_of(o), Cbo[...], base[2]))
 
+    def chunk(q):
+        return pl.ds(sum(SIZES[:q]), SIZES[q])
+
     def rows_of(k, q):
-        return pl.ds(pl.multiple_of(((y + k) % 4) * 320 + q * ROWS, ROWS), ROWS)
-
-    sides = (pl.ds(0, 128), pl.ds(128, 128))
+        return pl.ds(pl.multiple_of(((y + k) % 4) * PIECE + sum(SIZES[:q]), 16), SIZES[q])
+
     direct = {}
     for q in range(CHUNKS):
         direct[q] = group()
         for k in (2, 1, 3):
-            for i in range(2):
-                Ly[q, k - 1, i] = enc(L32[rows_of(k, q), sides[i]])
-            put(Ly.at[q, k - 1], Lr.at[q, k - 1], at_y(k), direct[q])
+            Ly[k - 1, chunk(q)] = enc(L32[rows_of(k, q)])
+            put(Ly.at[k - 1, chunk(q)], Lr.at[k - 1, chunk(q)], at_y(k), direct[q])
     ps = [group(), group()]
     bz = group()
     for i in range(2):
@@ -327,18 +331,18 @@
 
     def sum_l(q):
         wait(direct[q])
-        for i in range(2):
-            Lz[q, i] = enc(L32[rows_of(0, q), sides[i]] + dec(Lr[q, 0, i]) + dec(Lr[q, 1, i]) + dec(Lr[q, 2, i]))
-        zz[q] = put(Lz.at[q], Lzr.at[q], across)
+        at = chunk(q)
+        Lz[at] = enc(L32[rows_of(0, q)] + dec(Lr[0, at]) + dec(Lr[1, at]) + dec(Lr[2, at]))
+        zz[q] = put(Lz.at[at], Lzr.at[at], across)
 
     def share_l(q):
         wait(zz[q])
-        for i in range(2):
-            La[q, :, sides[i]] = enc(dec(Lz[q, i]) + dec(Lzr[q, i]))
+        at = chunk(q)
+        La[at] = enc(dec(Lz[at]) + dec(Lzr[at]))
         here = lg.at[rows_of(0, q)]
         for k in (2, 1, 3):
-            put(La.at[q], here, at_y(k), last)
-        kept.append(pltpu.make_async_copy(La.at[q], here, local.at[q]))
+            put(La.at[at], here, at_y(k), last)
+        kept.append(pltpu.make_async_copy(La.at[at], here, local.at[q]))
         kept[-1].start()
 
     pz = []
@@ -442,15 +446,15 @@
             V((3, 2, 8, PREST), BF16),
             V((8, PREST), F32),
             V((D_IN, BLOCK), F32),
-            V((CHUNKS, 3, 2, ROWS, 128), BF16),
-            V((CHUNKS, 3, 2, ROWS, 128), BF16),
-            V((CHUNKS, 2, ROWS, 128), BF16),
-            V((CHUNKS, 2, ROWS, 128), BF16),
-            V((CHUNKS, ROWS, BLOCK), BF16),
+            V((3, PIECE, BLOCK), BF16),
+            V((3, PIECE, BLOCK), BF16),
+            V((PIECE, BLOCK), BF16),
+            V((PIECE, BLOCK), BF16),
+            V((PIECE, BLOCK), BF16),
             V((10240, 128), F32),
             pltpu.SemaphoreType.DMA,
             pltpu.SemaphoreType.DMA((NGROUPS,)),
-            pltpu.SemaphoreType.DMA((4,)),
+            pltpu.SemaphoreType.DMA((CHUNKS,)),
             pltpu.SemaphoreType.REGULAR,
         ],
         compiler_params=pltpu.CompilerParams(
@@ -470,7 +474,7 @@
     )(ig, lg)
 
 
-NGROUPS = 40
+NGROUPS = 26 + CHUNKS
 VLIM = 24 * 2**20
 
 

time: 54.3 us -> 53.6 us (0.987)
  Pallas kernels: 53.5 us -> 52.9 us
    pallas_call x1, Pallas kernels: 52.3 us -> 51.6 us  [shards(): pl.pallas_call(kernel, out_shape=(jax.ShapeDtypeStruct((8, 2, D_IN), F32)...]
where the time goes in v6:
time: 53.6 us; the launch traced here: 53.5 us
  Pallas kernels  52.9 us (99%)
  between operations  0.64 us (1%)
    pallas_call x1, Pallas kernels, shards(): pl.pallas_call(kernel, out_shape=(jax.ShapeDtypeStruct((8, 2, D_IN), F32)...  51.6 us
    pallas_call x1, Pallas kernels, shards(): pl.pallas_call(finish, out_shape=(jax.ShapeDtypeStruct((8, 2, D_IN), F32)...  1.27 us

profile of v6, /device:TPU:8, one launch (start us, length us, event | category | flops | bytes accessed | tf_op | source)
XLA Modules:
  0.0 53.5 jit_solution(6867142313906242721)
XLA Ops:
  0.6 51.6 %shard_map.41 = (f32[8,2,1280]{2,1,0:T(2,128)S(1)}, bf16[1280,256]{1,0:T(8,128)(2,1)S(1)}) custom-call(bf16[8,2,1280]{2,1,0:T(2,128)(2,1)} %img.1, bf16[1280,256]{1,0:T(8,128)(2,1)} %w_hbm.1), custom_call_target="tpu_custom_call" | custom-call | tf_op jit(solution)/shard_map/pallas_call | solution.py:400
  52.3 1.3 %shard_map.42 = (f32[8,2,1280]{2,1,0:T(2,128)}, f32[1280,256]{1,0:T(8,128)}) custom-call(f32[8,2,1280]{2,1,0:T(2,128)S(1)} %get-tuple-element.4.ig, bf16[1280,256]{1,0:T(8,128)(2,1)S(1)} %get-tuple-element.5.lg), custom_call_target="tpu_custom_call" | custom-call | tf_op jit(solution)/shard_map/pallas_call | solution.py:464

commit v7 on v6

--- a/solution.py
+++ b/solution.py
@@ -19,7 +19,9 @@
 VAR = S * 25.0 / (EMB * (M - 1))
 COV = S * 4.0 / (EMB * (M - 1))
 PIECE = D_IN // 4
-SIZES = (64, 96, 96, 64)
+SIZES = (64, 96, 96)
+LATE = sum(SIZES)
+ZROWS = PIECE - LATE
 CHUNKS = len(SIZES)
 CUT = 896
 REST = D_IN - CUT
@@ -78,6 +80,7 @@
     P32, Pc, Px, S32, Pz, Pzr, So,
     B32, Bc, Bz, B2, Bx, Bxr, Bo,
     L32, Ly, Lr, Lz, Lzr, La,
+    Zc, Zr, H, Hc, Hr, Ht,
     span, send, recv, local, near,
 ):
     rep, dp = lax.axis_index("rep"), lax.axis_index("dp")
@@ -280,6 +283,14 @@
     def rows_of(k, q):
         return pl.ds(pl.multiple_of(((y + k) % 4) * PIECE + sum(SIZES[:q]), 16), SIZES[q])
 
+    def z_rows(piece):
+        return pl.ds(pl.multiple_of(piece * PIECE + LATE, 16), ZROWS)
+
+    mine_z = pl.ds(pl.multiple_of(zl * 128, 128), 128)
+    other_z = pl.ds(pl.multiple_of((1 - zl) * 128, 128), 128)
+    for p in range(4):
+        Zc[p] = enc(L32[z_rows(p), other_z])
+    za = put(Zc, Zr, across)
     direct = {}
     for q in range(CHUNKS):
         direct[q] = group()
@@ -345,7 +356,36 @@
         kept.append(pltpu.make_async_copy(La.at[at], here, local.at[q]))
         kept[-1].start()
 
+    zw = group()
+    zy = group()
+    zlast = group()
+
+    def z_first():
+        wait(za)
+        for p in range(4):
+            H[p] = L32[z_rows(p), mine_z] + dec(Zr[p])
+        for k in (2, 1, 3):
+            Hc[k - 1] = enc(H[(y + k) % 4])
+            put(Hc.at[k - 1], Hr.at[k - 1], at_y(k), zw)
+
+    def z_second():
+        wait(zw)
+        Ht[...] = enc(H[y] + dec(Hr[0]) + dec(Hr[1]) + dec(Hr[2]))
+        here = lg.at[z_rows(y), mine_z]
+        for k in (2, 1, 3):
+            put(Ht, here, at_y(k), zy)
+        put(Ht, here, across, zlast)
+        kept.append(pltpu.make_async_copy(Ht, here, local.at[CHUNKS]))
+        kept[-1].start()
+
+    def z_third():
+        wait(zy)
+        for k in (1, 2, 3):
+            there = lg.at[z_rows((y + k) % 4), mine_z]
+            put(there, there, across, zlast)
+
     pz = []
+    z_first()
     sum_l(0)
     sum_l(1)
     pz.append(sum_a(0))
@@ -353,10 +393,10 @@
     share_l(0)
     sum_l(2)
     pz.append(sum_a(1))
+    z_second()
     share_l(1)
-    sum_l(3)
     share_l(2)
-    share_l(3)
+    z_third()
 
     wait(mates)
     mine = at_core(c)
@@ -378,6 +418,7 @@
     ig[:, 1, :] = jnp.where(first, other, own)
 
     wait(last)
+    wait(zlast)
     for copy in kept:
         copy.wait()
     wait(sent)
@@ -446,15 +487,21 @@
             V((3, 2, 8, PREST), BF16),
             V((8, PREST), F32),
             V((D_IN, BLOCK), F32),
-            V((3, PIECE, BLOCK), BF16),
-            V((3, PIECE, BLOCK), BF16),
-            V((PIECE, BLOCK), BF16),
-            V((PIECE, BLOCK), BF16),
-            V((PIECE, BLOCK), BF16),
+            V((3, LATE, BLOCK), BF16),
+            V((3, LATE, BLOCK), BF16),
+            V((LATE, BLOCK), BF16),
+            V((LATE, BLOCK), BF16),
+            V((LATE, BLOCK), BF16),
+            V((4, ZROWS, 128), BF16),
+            V((4, ZROWS, 128), BF16),
+            V((4, ZROWS, 128), F32),
+            V((3, ZROWS, 128), BF16),
+            V((3, ZROWS, 128), BF16),
+            V((ZROWS, 128), BF16),
             V((10240, 128), F32),
             pltpu.SemaphoreType.DMA,
             pltpu.SemaphoreType.DMA((NGROUPS,)),
-            pltpu.SemaphoreType.DMA((CHUNKS,)),
+            pltpu.SemaphoreType.DMA((CHUNKS + 1,)),
             pltpu.SemaphoreType.REGULAR,
         ],
         compiler_params=pltpu.CompilerParams(
@@ -474,7 +521,7 @@
     )(ig, lg)
 
 
-NGROUPS = 26 + CHUNKS
+NGROUPS = 30 + CHUNKS
 VLIM = 24 * 2**20
 
 

time: 53.6 us -> 53.1 us (level)
  Pallas kernels: 52.9 us -> 51.9 us
    pallas_call x1, Pallas kernels: 51.6 us -> 50.6 us  [shards(): pl.pallas_call(kernel, out_shape=(jax.ShapeDtypeStruct((8, 2, D_IN), F32)...]
where the time goes in v7:
time: 53.1 us; the launch traced here: 52.5 us
  Pallas kernels  51.9 us (98%)
  between operations  0.64 us (1%)
    pallas_call x1, Pallas kernels, shards(): pl.pallas_call(kernel, out_shape=(jax.ShapeDtypeStruct((8, 2, D_IN), F32)...  50.6 us
    pallas_call x1, Pallas kernels, shards(): pl.pallas_call(finish, out_shape=(jax.ShapeDtypeStruct((8, 2, D_IN), F32)...  1.27 us

profile of v7, /device:TPU:8, one launch (start us, length us, event | category | flops | bytes accessed | tf_op | source)
XLA Modules:
  0.0 52.5 jit_solution(7022349793649727316)
XLA Ops:
  0.6 50.6 %shard_map.41 = (f32[8,2,1280]{2,1,0:T(2,128)S(1)}, bf16[1280,256]{1,0:T(8,128)(2,1)S(1)}) custom-call(bf16[8,2,1280]{2,1,0:T(2,128)(2,1)} %img.1, bf16[1280,256]{1,0:T(8,128)(2,1)} %w_hbm.1), custom_call_target="tpu_custom_call" | custom-call | tf_op jit(solution)/shard_map/pallas_call | solution.py:441
  51.3 1.3 %shard_map.42 = (f32[8,2,1280]{2,1,0:T(2,128)}, f32[1280,256]{1,0:T(8,128)}) custom-call(f32[8,2,1280]{2,1,0:T(2,128)S(1)} %get-tuple-element.4.ig, bf16[1280,256]{1,0:T(8,128)(2,1)S(1)} %get-tuple-element.5.lg), custom_call_target="tpu_custom_call" | custom-call | tf_op jit(solution)/shard_map/pallas_call | solution.py:511

commit v8 on v7

--- a/solution.py
+++ b/solution.py
@@ -23,7 +23,7 @@
 LATE = sum(SIZES)
 ZROWS = PIECE - LATE
 CHUNKS = len(SIZES)
-CUT = 896
+CUT = 1024
 REST = D_IN - CUT
 PCUT = 1024
 PREST = D_IN - PCUT
@@ -107,11 +107,10 @@
     wfetch = pltpu.make_async_copy(w_hbm, w, local.at[1])
     wfetch.start()
     barrier = pltpu.get_barrier_semaphore()
-    peers = [partner, across]
-    for k in (1, 2, 3):
+    peers = [at_z(k, core) for k in (1, 3) for core in (c, o)]
+    for k in (2, 1, 3):
         peers += [at_x(k, c), at_x(k, o), at_y(k)]
-    for k in (1, 3):
-        peers += [at_z(k, c), at_z(k, o)]
+    peers += [across, partner]
     for peer in peers:
         pl.semaphore_signal(barrier, inc=1, device_id=peer, device_id_type=MESH)
     fetch.wait()
@@ -166,7 +165,7 @@
     pl.semaphore_wait(near, 1)
     for core in (c, o):
         put(I2.at[core, :, A], X.at[chip, at, A], at_z(2, core), az[2])
-    for name, k in (("A", 0), ("B", 0), ("B", 1), ("B", 3), ("A", 1), ("A", 3), ("B", 2), ("A", 2)):
+    for name, k in (("A", 0), ("A", 1), ("A", 3), ("B", 0), ("B", 1), ("B", 3), ("B", 2), ("A", 2)):
         if name == "A":
             if k:
                 wait(az[k])
@@ -181,8 +180,8 @@
                 put(X.at[slot, :, B], X.at[slot, :, B], at_z(j, c), forwards)
     wait(wswap)
     wfetch.wait()
-    WT[0] = w[...].T
-    WT[1] = Wo[...].T
+    WT[0:BLOCK] = w[...].T
+    WT[BLOCK:2 * BLOCK] = Wo[...].T
     wait(forwards)
     xswap = put(X, Xo, partner)
 
@@ -262,17 +261,18 @@
         return (rest + through * (COV / (M - 1))).astype(BF16)
 
     gram = gram_of(c)
-    Ff[0] = feature_grad(gram, Cb[:, 0:BLOCK], base[0])
-    Ff[1] = feature_grad(gram, Cb[:, BLOCK:2 * BLOCK], base[1])
-    part = nn(Ff[0], WT[0]) + nn(Ff[1], WT[1])
-    P32[...] = part[:, 0:PCUT].reshape(4, 4, 16, PCUT)
+    Ff[:, 0:BLOCK] = feature_grad(gram, Cb[:, 0:BLOCK], base[0])
+    Ff[:, BLOCK:2 * BLOCK] = feature_grad(gram, Cb[:, BLOCK:2 * BLOCK], base[1])
+    part = nn(Ff[...], WT[...])
+    main = part[:, 0:PCUT].reshape(4, 4, 16, PCUT)
+    P32[...] = main
+    Pc[...] = enc(main)
     part = part[:, PCUT:D_IN].reshape(4, 4, 16, PREST)
     halves = (pl.ds(0, PCUT // 2), pl.ds(PCUT // 2, PCUT // 2))
-    Pc[...] = enc(P32[...])
     for j in range(4):
         B32[j] = part[:, j]
         Bc[j] = enc(part[:, j])
-    L32[...] = nn(XT[0], Ff[0])
+    L32[...] = nn(XT[0], Ff[:, 0:BLOCK])
 
     wait(go)
     L32[...] += nn(XT[1], feature_grad(gram_of(o), Cbo[...], base[2]))
@@ -454,7 +454,7 @@
             V((16, 16, D_IN), BF16),
             V((2, D_IN, M), BF16),
             V((D_IN, BLOCK), BF16),
-            V((2, BLOCK, D_IN), BF16),
+            V((2 * BLOCK, D_IN), BF16),
             V((2, M, BLOCK), F32),
             V((M, 2 * BLOCK), BF16),
             V((M, BLOCK), BF16),
@@ -471,7 +471,7 @@
             V((8, 128), F32),
             V((3, 8, 128), F32),
             V((2, 8, 128), F32),
-            V((2, M, BLOCK), BF16),
+            V((M, 2 * BLOCK), BF16),
             V((4, 4, 16, PCUT), F32),
             V((4, 4, 16, PCUT), BF16),
             V((3, 4, 16, PCUT), BF16),

time: 53.1 us -> 52.6 us (level)
  no operation moved by 1% of the time
where the time goes in v8:
time: 52.6 us; the launch traced here: 52.5 us
  Pallas kernels  51.8 us (98%)
  between operations  0.64 us (1%)
    pallas_call x1, Pallas kernels, shards(): pl.pallas_call(kernel, out_shape=(jax.ShapeDtypeStruct((8, 2, D_IN), F32)...  50.6 us
    pallas_call x1, Pallas kernels, shards(): pl.pallas_call(finish, out_shape=(jax.ShapeDtypeStruct((8, 2, D_IN), F32)...  1.27 us

profile of v8, /device:TPU:8, one launch (start us, length us, event | category | flops | bytes accessed | tf_op | source)
XLA Modules:
  0.0 52.5 jit_solution(14370931633787908459)
XLA Ops:
  0.6 50.6 %shard_map.41 = (f32[8,2,1280]{2,1,0:T(2,128)S(1)}, bf16[1280,256]{1,0:T(8,128)(2,1)S(1)}) custom-call(bf16[8,2,1280]{2,1,0:T(2,128)(2,1)} %img.1, bf16[1280,256]{1,0:T(8,128)(2,1)} %w_hbm.1), custom_call_target="tpu_custom_call" | custom-call | tf_op jit(solution)/shard_map/pallas_call | solution.py:441
  51.2 1.3 %shard_map.42 = (f32[8,2,1280]{2,1,0:T(2,128)}, f32[1280,256]{1,0:T(8,128)}) custom-call(f32[8,2,1280]{2,1,0:T(2,128)S(1)} %get-tuple-element.4.ig, bf16[1280,256]{1,0:T(8,128)(2,1)S(1)} %get-tuple-element.5.lg), custom_call_target="tpu_custom_call" | custom-call | tf_op jit(solution)/shard_map/pallas_call | solution.py:511

commit v9 on v8

--- a/solution.py
+++ b/solution.py
@@ -162,9 +162,6 @@
     keep.wait()
     wait(mate)
     forwards = group()
-    pl.semaphore_wait(near, 1)
-    for core in (c, o):
-        put(I2.at[core, :, A], X.at[chip, at, A], at_z(2, core), az[2])
     for name, k in (("A", 0), ("A", 1), ("A", 3), ("B", 0), ("B", 1), ("B", 3), ("B", 2), ("A", 2)):
         if name == "A":
             if k:
@@ -172,6 +169,10 @@
             slot = x * 4 + (zh - k + 4) % 4
             for j in (2, 1, 3):
                 put(X.at[slot, :, A], X.at[slot, :, A], at_x(j, c), forwards)
+            if k == 0:
+                pl.semaphore_wait(near, 1)
+                for core in (c, o):
+                    put(I2.at[core, :, A], X.at[chip, at, A], at_z(2, core), az[2])
         else:
             if k:
                 wait(bx[k])

time: 52.6 us -> 52.4 us (level)
  no operation moved by 1% of the time
where the time goes in v9:
time: 52.4 us; the launch traced here: 52 us
  Pallas kernels  51.4 us (98%)
  between operations  0.64 us (1%)
    pallas_call x1, Pallas kernels, shards(): pl.pallas_call(kernel, out_shape=(jax.ShapeDtypeStruct((8, 2, D_IN), F32)...  50.1 us
    pallas_call x1, Pallas kernels, shards(): pl.pallas_call(finish, out_shape=(jax.ShapeDtypeStruct((8, 2, D_IN), F32)...  1.27 us

profile of v9, /device:TPU:8, one launch (start us, length us, event | category | flops | bytes accessed | tf_op | source)
XLA Modules:
  0.0 52.0 jit_solution(4037669803749159582)
XLA Ops:
  0.6 50.1 %shard_map.41 = (f32[8,2,1280]{2,1,0:T(2,128)S(1)}, bf16[1280,256]{1,0:T(8,128)(2,1)S(1)}) custom-call(bf16[8,2,1280]{2,1,0:T(2,128)(2,1)} %img.1, bf16[1280,256]{1,0:T(8,128)(2,1)} %w_hbm.1), custom_call_target="tpu_custom_call" | custom-call | tf_op jit(solution)/shard_map/pallas_call | solution.py:442
  50.8 1.3 %shard_map.42 = (f32[8,2,1280]{2,1,0:T(2,128)}, f32[1280,256]{1,0:T(8,128)}) custom-call(f32[8,2,1280]{2,1,0:T(2,128)S(1)} %get-tuple-element.4.ig, bf16[1280,256]{1,0:T(8,128)(2,1)S(1)} %get-tuple-element.5.lg), custom_call_target="tpu_custom_call" | custom-call | tf_op jit(solution)/shard_map/pallas_call | solution.py:512
